TPU v7x, 256 devices: a whole 4x4x8 slice. The times are simulated.
256 devices in a mesh: expert: 64 (over z, x, core), dp: 4 (over y).
Axes of the slice: x: 4, y: 4, z: 8, core: 2. Of those that a mesh axis runs over, the one named last changes fastest.
Arguments:
- tokens: bfloat16 [32768, 2048], P(('expert', 'dp')), may hold values from -6 to 6
- expert_ids: int32 [32768, 2], P(('expert', 'dp')), may hold values from 0 to 63, all different within a row; in each aligned block of 128 rows (0 to 127, 128 to 255, ...) at most 6 rows name the same one
- gate_scores: float32 [32768, 2], P(('expert', 'dp')), may hold values from 0.2 to 1
- gate_proj: bfloat16 [64, 768, 2048], P('expert', 'dp'), may hold values from -0.125 to 0.125
- up_proj: bfloat16 [64, 768, 2048], P('expert', 'dp'), may hold values from -0.125 to 0.125
- down_proj: bfloat16 [64, 768, 2048], P('expert', 'dp'), may hold values from -0.21875 to 0.21875
- out_grad: bfloat16 [32768, 2048], P(('expert', 'dp')), may hold values from -0.59765625 to 0.59765625
Outputs:
- output: bfloat16 [32768, 2048], P(('expert', 'dp'))
- d_tokens: bfloat16 [32768, 2048], P(('expert', 'dp'))
- d_scores: float32 [32768, 2], P(('expert', 'dp'))
- d_gate_proj: bfloat16 [64, 768, 2048], P('expert', 'dp')
- d_up_proj: bfloat16 [64, 768, 2048], P('expert', 'dp')
- d_down_proj: bfloat16 [64, 768, 2048], P('expert', 'dp')
Inputs may be any that keep to these rules, and one draw needn't show every extreme that they name: `expert_ids`: each token names 2 different experts. Among the routes of one device's 128 tokens no expert is named more than 6 times, and in some devices' blocks some expert is named exactly 6 times.
All inputs are finite; a program needn't handle non-finite values.
Results may differ from a plain program's by a relative error of at most 0.014.
Values may be sent and summed in bfloat16 or wider, within the bound.
A program may use at most 128 MiB of HBM per device.

v0:
```python
import jax
import jax.numpy as jnp
from jax import lax
from jax.sharding import PartitionSpec as P


def sent_together(arrays, axis, dim, along):
    widths = [a.shape[along] for a in arrays]
    both = jnp.concatenate(arrays, axis=along)
    filled = lax.all_gather(both, axis, axis=dim, tiled=True)
    return tuple(jnp.split(filled, [sum(widths[:k]) for k in range(1, len(widths))], axis=along))


def silu_parts(preact):
    logistic = jax.nn.sigmoid(preact)
    return (preact * logistic, logistic * (1.0 + preact * (1.0 - logistic)))


def scatter_slots(values, target, slot_total):
    return jnp.zeros((slot_total, values.shape[1]), values.dtype).at[target].set(values)


def shards(tokens, expert_ids, gate_scores, gate_proj, up_proj, down_proj, out_grad):
    tok_count, model_width = tokens.shape
    routes_per = expert_ids.shape[1]
    experts = lax.axis_size("expert")
    capacity = max(2, 3 * tok_count * routes_per // (2 * experts))
    slot_total = experts * capacity
    flat_ids = expert_ids.reshape(-1)
    onehot = (flat_ids[:, None] == jnp.arange(experts, dtype=jnp.int32)[None, :]).astype(jnp.int32)
    position = jnp.sum(jnp.cumsum(onehot, axis=0) * onehot, axis=1) - 1
    target = flat_ids * capacity + position
    outgoing = scatter_slots(jnp.repeat(tokens, routes_per, axis=0), target, slot_total)
    received = lax.all_to_all(
        outgoing.reshape(experts, capacity, model_width),
        "expert",
        split_axis=0,
        concat_axis=0,
        tiled=True,
    )
    received = received.reshape(slot_total, model_width)
    gate_full, up_full, down_full = sent_together((gate_proj, up_proj, down_proj), "dp", 1, 0)
    gate_w = gate_full[0]
    up_w = up_full[0]
    down_w = down_full[0]
    gate_pre = jnp.dot(received, gate_w.T, preferred_element_type=jnp.float32)
    up_pre = jnp.dot(received, up_w.T, preferred_element_type=jnp.float32)
    activated, silu_slope = silu_parts(gate_pre)
    hidden = (activated * up_pre).astype(jnp.bfloat16)
    expert_out = jnp.dot(hidden, down_w, preferred_element_type=jnp.float32).astype(jnp.bfloat16)
    returned = lax.all_to_all(
        expert_out.reshape(experts, capacity, model_width),
        "expert",
        split_axis=0,
        concat_axis=0,
        tiled=True,
    )
    pair_out = returned.reshape(slot_total, model_width)[target].astype(jnp.float32)
    scores = gate_scores.reshape(-1, 1)
    output = jnp.sum(
        (scores * pair_out).reshape(tok_count, routes_per, model_width), axis=1
    ).astype(jnp.bfloat16)
    pair_grad = jnp.repeat(out_grad, routes_per, axis=0).astype(jnp.float32)
    d_scores = jnp.sum(pair_grad * pair_out, axis=1).reshape(tok_count, routes_per)
    out_cot = (scores * pair_grad).astype(jnp.bfloat16)
    cot_slots = scatter_slots(out_cot, target, slot_total)
    cot_rows = lax.all_to_all(
        cot_slots.reshape(experts, capacity, model_width),
        "expert",
        split_axis=0,
        concat_axis=0,
        tiled=True,
    )
    cot_rows = cot_rows.reshape(slot_total, model_width)
    hidden_grad = jnp.dot(cot_rows, down_w.T, preferred_element_type=jnp.float32)
    gate_grad = (hidden_grad * up_pre * silu_slope).astype(jnp.bfloat16)
    up_grad = (hidden_grad * activated).astype(jnp.bfloat16)
    input_grad = (
        jnp.dot(gate_grad, gate_w, preferred_element_type=jnp.float32)
        + jnp.dot(up_grad, up_w, preferred_element_type=jnp.float32)
    ).astype(jnp.bfloat16)
    grad_terms = (
        jnp.dot(gate_grad.T, received, preferred_element_type=jnp.float32)[None],
        jnp.dot(up_grad.T, received, preferred_element_type=jnp.float32)[None],
        jnp.dot(hidden.T, cot_rows, preferred_element_type=jnp.float32)[None],
    )
    gate_sum, up_sum, down_sum = (
        lax.psum_scatter(
            grad_terms[0].astype(jnp.bfloat16), "dp", scatter_dimension=1, tiled=True
        ).astype(jnp.float32),
        lax.psum_scatter(
            grad_terms[1].astype(jnp.bfloat16), "dp", scatter_dimension=1, tiled=True
        ).astype(jnp.float32),
        lax.psum_scatter(
            grad_terms[2].astype(jnp.bfloat16), "dp", scatter_dimension=1, tiled=True
        ).astype(jnp.float32),
    )
    gate_out = gate_sum.astype(jnp.bfloat16)
    up_out = up_sum.astype(jnp.bfloat16)
    down_out = down_sum.astype(jnp.bfloat16)
    returned_grad = lax.all_to_all(
        input_grad.reshape(experts, capacity, model_width),
        "expert",
        split_axis=0,
        concat_axis=0,
        tiled=True,
    )
    pair_input = returned_grad.reshape(slot_total, model_width)[target].astype(jnp.float32)
    d_tokens = jnp.sum(pair_input.reshape(tok_count, routes_per, model_width), axis=1).astype(
        jnp.bfloat16
    )
    return (output, d_tokens, d_scores, gate_out, up_out, down_out)


def solution(mesh):
    in_specs = (
        P(("expert", "dp"), None),
        P(("expert", "dp"), None),
        P(("expert", "dp"), None),
        P("expert", "dp", None),
        P("expert", "dp", None),
        P("expert", "dp", None),
        P(("expert", "dp"), None),
    )
    out_specs = (
        P(("expert", "dp"), None),
        P(("expert", "dp"), None),
        P(("expert", "dp"), None),
        P("expert", "dp", None),
        P("expert", "dp", None),
        P("expert", "dp", None),
    )
    return jax.shard_map(shards, mesh=mesh, in_specs=in_specs, out_specs=out_specs, check_vma=False)
```

profile of v0, /device:TPU:1, one launch (start us, length us, event | category | flops | bytes accessed | tf_op | source)
XLA Modules:
  0.0 300.1 jit_solution(16909950419331906807)
XLA Ops:
  7.2 3.3 %pad_maximum_fusion = bf16[3,192,2048]{2,1,0:T(8,128)(2,1)} fusion(bf16[1,192,2048]{2,1,0:T(8,128)(2,1)} %param.12, bf16[1,192,2048]{2,1,0:T(8,128)(2,1)} %param.11, bf16[1,192,2048]{2,1,0:T(8,128)(2,1)} %param.10), kind=kLoop, calls=%fused_computation.19 | loop fusion | flops 2359296 | bytes 4718592 | tf_op jit(solution)/shard_map/concatenate | solution.py:9
  13.9 2.6 scatter_custom_fusion
  16.5 1.6 reshape.121
  18.1 13.3 %all-to-all-start = ((bf16[64,6,2048]{2,1,0:T(8,128)(2,1)}), bf16[64,6,2048]{2,1,0:T(8,128)(2,1)}, u32[]{:S(2)}, u32[]{:S(2)}) async-start(bf16[64,6,2048]{2,1,0:T(8,128)(2,1)} %reshape.121), calls=%async_computation | async-start | bytes 4194304 | tf_op jit(solution)/shard_map/all_to_all | solution.py:34
  31.7 2.4 broadcast_in_dim.5
  34.1 2.7 convert_element_type.82
  36.8 3.5 %scatter_custom_fusion.1 = bf16[384,2048]{1,0:T(8,128)(2,1)} fusion(s32[256]{0:T(256)S(1)} %bitcast.52, f32[256,2048]{1,0:T(8,128)S(1)} %convert_element_type.82, f32[256]{0:T(256)S(1)} %mul.74, bf16[]{:T(256)} %constant.7.clone.1), kind=kCustom, calls=%fused_computation.28 | custom fusion | flops 1048576 | bytes 3671042 | tf_op jit(solution)/shard_map/scatter | solution.py:20
  40.3 3.7 %reshape.125 = bf16[64,6,2048]{2,1,0:T(8,128)(2,1)} reshape(bf16[384,2048]{1,0:T(8,128)(2,1)} %scatter_custom_fusion.1) | data formatting | bytes 3145728 | tf_op jit(solution)/shard_map/reshape | solution.py:68
  44.0 37.0 %all-to-all-done = bf16[64,6,2048]{2,1,0:T(8,128)(2,1)} async-done(((bf16[64,6,2048]{2,1,0:T(8,128)(2,1)}), bf16[64,6,2048]{2,1,0:T(8,128)(2,1)}, u32[]{:S(2)}, u32[]{:S(2)}) %all-to-all-start) | async-done | bytes 1572896 | tf_op jit(solution)/shard_map/all_to_all | solution.py:34
  81.0 7.0 %all-to-all-start.2 = ((bf16[64,6,2048]{2,1,0:T(8,128)(2,1)}), bf16[64,6,2048]{2,1,0:T(8,128)(2,1)S(1)}, u32[]{:S(2)}, u32[]{:S(2)}) async-start(bf16[64,6,2048]{2,1,0:T(8,128)(2,1)} %reshape.125), calls=%async_computation.2 | async-start | bytes 4194304 | tf_op jit(solution)/shard_map/all_to_all | solution.py:67
  88.2 3.7 %reshape.122 = bf16[384,2048]{1,0:T(8,128)(2,1)} reshape(bf16[64,6,2048]{2,1,0:T(8,128)(2,1)} %all-to-all-done) | data formatting | bytes 3145728 | tf_op jit(solution)/shard_map/reshape | solution.py:41
  91.9 45.8 %all-to-all-done.2 = bf16[64,6,2048]{2,1,0:T(8,128)(2,1)S(1)} async-done(((bf16[64,6,2048]{2,1,0:T(8,128)(2,1)}), bf16[64,6,2048]{2,1,0:T(8,128)(2,1)S(1)}, u32[]{:S(2)}, u32[]{:S(2)}) %all-to-all-start.2) | async-done | bytes 1572896 | tf_op jit(solution)/shard_map/all_to_all | solution.py:67
  139.2 3.9 %fusion.5 = f32[384,768]{1,0:T(8,128)S(1)} fusion(bf16[384,2048]{1,0:T(8,128)(2,1)} %reshape.122, bf16[3,768,2048]{2,1,0:T(8,128)(2,1)} %all-gather.2.cloned.1.call-done), kind=kOutput, calls=%fused_computation.17 | convolution fusion | flops 1207959552 | bytes 5898240 | tf_op jit(solution)/shard_map/dot_general | solution.py:47
  143.1 3.4 %fusion.4 = f32[384,768]{1,0:T(8,128)S(1)} fusion(bf16[384,2048]{1,0:T(8,128)(2,1)S(1)} %copy-done.4, bf16[3,768,2048]{2,1,0:T(8,128)(2,1)} %all-gather.2.cloned.1.call-done), kind=kOutput, calls=%fused_computation.16 | convolution fusion | flops 1207959552 | bytes 5898240 | tf_op jit(solution)/shard_map/dot_general | solution.py:46
  146.5 4.5 %multiply_convert_fusion.1 = (bf16[384,768]{1,0:T(8,128)(2,1)S(1)}, bf16[384,768]{1,0:T(8,128)(2,1)}, bf16[384,768]{1,0:T(8,128)(2,1)S(1)}) fusion(f32[384,768]{1,0:T(8,128)S(1)} %fusion.4, f32[384,768]{1,0:T(8,128)S(1)} %fusion.5, bf16[384,2048]{1,0:T(8,128)(2,1)S(1)} %copy-done.5, bf16[3,768,2048]{2,1,0:T(8,128)(2,1)} %all-gather.2.cloned.1.call-done), kind=kOutput, calls=%fused_computation.23 | convolution fusion | flops 1212383232 | bytes 8847360 | tf_op jit(solution)/shard_map/dot_general | solution.py:75
  151.8 3.5 %fusion.2 = bf16[1,768,2048]{2,1,0:T(8,128)(2,1)} fusion(bf16[384,768]{1,0:T(8,128)(2,1)S(1)} %get-tuple-element.14, bf16[384,2048]{1,0:T(8,128)(2,1)S(1)} %copy-done.5), kind=kOutput, calls=%fused_computation.13 | convolution fusion | flops 1209532416 | bytes 5308416 | tf_op jit(solution)/shard_map/dot_general | solution.py:85
  155.4 3.5 %fusion.1 = bf16[1,768,2048]{2,1,0:T(8,128)(2,1)} fusion(bf16[384,768]{1,0:T(8,128)(2,1)S(1)} %get-tuple-element.12, bf16[384,2048]{1,0:T(8,128)(2,1)S(1)} %copy-done.4), kind=kOutput, calls=%fused_computation.12 | convolution fusion | flops 1209532416 | bytes 5308416 | tf_op jit(solution)/shard_map/dot_general | solution.py:84
  159.9 3.3 %convolution_convert_fusion.3 = bf16[384,2048]{1,0:T(8,128)(2,1)S(1)} fusion(bf16[384,768]{1,0:T(8,128)(2,1)S(1)} %copy-done.13, bf16[3,768,2048]{2,1,0:T(8,128)(2,1)} %all-gather.2.cloned.1.call-done), kind=kOutput, calls=%fused_computation.14 | convolution fusion | flops 1208745984 | bytes 5308416 | tf_op jit(solution)/shard_map/dot_general | solution.py:50
  163.2 1.6 reshape.123
  164.8 7.0 %all-to-all-start.1 = ((bf16[64,6,2048]{2,1,0:T(8,128)(2,1)}), bf16[64,6,2048]{2,1,0:T(8,128)(2,1)S(1)}, u32[]{:S(2)}, u32[]{:S(2)}) async-start(bf16[64,6,2048]{2,1,0:T(8,128)(2,1)} %reshape.123), calls=%async_computation.1 | async-start | bytes 4194304 | tf_op jit(solution)/shard_map/all_to_all | solution.py:51
  172.1 5.1 %fusion = bf16[1,768,2048]{2,1,0:T(8,128)(2,1)} fusion(bf16[384,768]{1,0:T(8,128)(2,1)} %get-tuple-element.13, bf16[384,2048]{1,0:T(8,128)(2,1)} %reshape.122), kind=kOutput, calls=%fused_computation.11 | convolution fusion | flops 1209532416 | bytes 5308416 | tf_op jit(solution)/shard_map/dot_general | solution.py:83
  177.2 3.5 %fusion.3 = f32[384,2048]{1,0:T(8,128)S(1)} fusion(bf16[384,768]{1,0:T(8,128)(2,1)} %get-tuple-element.13, bf16[3,768,2048]{2,1,0:T(8,128)(2,1)} %all-gather.2.cloned.1.call-done), kind=kOutput, calls=%fused_computation.15 | convolution fusion | flops 1207959552 | bytes 6881280 | tf_op jit(solution)/shard_map/dot_general | solution.py:79
  180.8 4.5 %add_convert_fusion = bf16[384,2048]{1,0:T(8,128)(2,1)} fusion(f32[384,2048]{1,0:T(8,128)S(1)} %fusion.3, bf16[384,768]{1,0:T(8,128)(2,1)S(1)} %copy-done.11, bf16[3,768,2048]{2,1,0:T(8,128)(2,1)} %all-gather.2.cloned.1.call-done), kind=kOutput, calls=%fused_computation.10 | convolution fusion | flops 1209532416 | bytes 8454144 | tf_op jit(solution)/shard_map/dot_general | solution.py:80
  185.3 3.7 %reshape.127 = bf16[64,6,2048]{2,1,0:T(8,128)(2,1)} reshape(bf16[384,2048]{1,0:T(8,128)(2,1)} %add_convert_fusion) | data formatting | bytes 3145728 | tf_op jit(solution)/shard_map/reshape | solution.py:102
  189.1 32.5 %all-to-all-done.1 = bf16[64,6,2048]{2,1,0:T(8,128)(2,1)S(1)} async-done(((bf16[64,6,2048]{2,1,0:T(8,128)(2,1)}), bf16[64,6,2048]{2,1,0:T(8,128)(2,1)S(1)}, u32[]{:S(2)}, u32[]{:S(2)}) %all-to-all-start.1) | async-done | bytes 1572896 | tf_op jit(solution)/shard_map/all_to_all | solution.py:51
  222.8 7.2 %all-to-all-start.3 = ((bf16[64,6,2048]{2,1,0:T(8,128)(2,1)}), bf16[64,6,2048]{2,1,0:T(8,128)(2,1)}, u32[]{:S(2)}, u32[]{:S(2)}) async-start(bf16[64,6,2048]{2,1,0:T(8,128)(2,1)} %reshape.127), calls=%async_computation.3 | async-start | bytes 4194304 | tf_op jit(solution)/shard_map/all_to_all | solution.py:101
  230.0 2.6 reshape.124
  234.0 2.3 reshape.129
  237.4 42.2 %all-to-all-done.3 = bf16[64,6,2048]{2,1,0:T(8,128)(2,1)} async-done(((bf16[64,6,2048]{2,1,0:T(8,128)(2,1)}), bf16[64,6,2048]{2,1,0:T(8,128)(2,1)}, u32[]{:S(2)}, u32[]{:S(2)}) %all-to-all-start.3) | async-done | bytes 1572896 | tf_op jit(solution)/shard_map/all_to_all | solution.py:101
  279.6 2.6 reshape.128
  285.1 4.6 %reduce_sum.43 = bf16[128,2048]{1,0:T(8,128)(2,1)} reduce(bf16[128,2,2048]{2,1,0:T(2,128)(2,1)} %gather.10, bf16[]{:T(256)} %constant.7.clone.1), dimensions={1}, to_apply=%region_6.7 | reduce | flops 262144 | bytes 1572866 | tf_op jit(solution)/shard_map/reduce_sum | solution.py:109
  289.7 3.9 %multiply_reduce_fusion.1 = bf16[128,2048]{1,0:T(8,128)(2,1)} fusion(f32[128,2,2048]{2,1,0:T(2,128)S(1)} %copy-done.3, f32[128,2]{1,0:T(8,128)S(1)} %copy.14), kind=kLoop, calls=%fused_computation.22 | loop fusion | flops 786432 | bytes 2622464 | tf_op jit(solution)/shard_map/reduce_sum | solution.py:60
  (66 shorter events, 14.1 us)
Async XLA Ops:
  7.2 132.0 %all-gather.2.cloned.1.call-start = ((), (), s32[]{:S(2)}) async-start(), calls=%async_computation.7 | async-start | bytes 11796480 | tf_op jit(solution)/shard_map/all_gather | solution.py:10
  10.5 0.7 copy-start.8
  10.5 2.2 copy-start.6
  18.1 13.3 %copy-start.9 = (f32[128,2]{0,1:T(2,128)S(1)}, f32[128,2]{0,1:T(2,128)}, u32[]{:S(2)}) copy-start(f32[128,2]{0,1:T(2,128)} %param.9) | copy-start | bytes 3076
  18.1 13.6 %copy-start.7 = (bf16[128,2048]{1,0:T(8,128)(2,1)S(1)}, bf16[128,2048]{1,0:T(8,128)(2,1)}, u32[]{:S(2)}) copy-start(bf16[128,2048]{1,0:T(8,128)(2,1)} %param.13) | copy-start | bytes 1572868
  18.1 62.9 %all-to-all-start = ((bf16[64,6,2048]{2,1,0:T(8,128)(2,1)}), bf16[64,6,2048]{2,1,0:T(8,128)(2,1)}, u32[]{:S(2)}, u32[]{:S(2)}) async-start(bf16[64,6,2048]{2,1,0:T(8,128)(2,1)} %reshape.121), calls=%async_computation | async-start | bytes 4194304 | tf_op jit(solution)/shard_map/all_to_all | solution.py:34
  36.8 7.3 %copy-start = (f32[256,2048]{1,0:T(8,128)}, f32[256,2048]{1,0:T(8,128)S(1)}, u32[]{:S(2)}) copy-start(f32[256,2048]{1,0:T(8,128)S(1)} %convert_element_type.82) | copy-start | bytes 6291460
  81.0 56.7 %all-to-all-start.2 = ((bf16[64,6,2048]{2,1,0:T(8,128)(2,1)}), bf16[64,6,2048]{2,1,0:T(8,128)(2,1)S(1)}, u32[]{:S(2)}, u32[]{:S(2)}) async-start(bf16[64,6,2048]{2,1,0:T(8,128)(2,1)} %reshape.125), calls=%async_computation.2 | async-start | bytes 4194304 | tf_op jit(solution)/shard_map/all_to_all | solution.py:67
  88.0 205.6 %reduce-scatter.8.cloned.1.call-start = ((), (), s32[]{:S(2)}) async-start(), calls=%async_computation.10 | async-start | bytes 3932160 | tf_op jit(solution)/shard_map/reduce_scatter | solution.py:94
  139.2 3.9 %copy-start.4 = (bf16[384,2048]{1,0:T(8,128)(2,1)S(1)}, bf16[384,2048]{1,0:T(8,128)(2,1)}, u32[]{:S(2)}) copy-start(bf16[384,2048]{1,0:T(8,128)(2,1)} %reshape.122) | copy-start | bytes 4718596
  143.1 3.4 %copy-start.5 = (bf16[384,2048]{1,0:T(8,128)(2,1)S(1)}, bf16[384,2048]{1,0:T(8,128)(2,1)}, u32[]{:S(2)}) copy-start(bf16[384,2048]{1,0:T(8,128)(2,1)} %reshape.126) | copy-start | bytes 4718596
  151.0 0.8 copy-start.12
  151.0 4.4 %copy-start.10 = (bf16[384,768]{1,0:T(8,128)(2,1)}, bf16[384,768]{1,0:T(8,128)(2,1)S(1)}, u32[]{:S(2)}) copy-start(bf16[384,768]{1,0:T(8,128)(2,1)S(1)} %get-tuple-element.12) | copy-start | bytes 1769476
  155.3 138.3 %reduce-scatter.6.cloned.1.call-start = ((), (), s32[]{:S(2)}) async-start(), calls=%async_computation.9 | async-start | bytes 3932160 | tf_op jit(solution)/shard_map/reduce_scatter | solution.py:91
  158.9 1.1 copy-start.13
  164.8 56.7 %all-to-all-start.1 = ((bf16[64,6,2048]{2,1,0:T(8,128)(2,1)}), bf16[64,6,2048]{2,1,0:T(8,128)(2,1)S(1)}, u32[]{:S(2)}, u32[]{:S(2)}) async-start(bf16[64,6,2048]{2,1,0:T(8,128)(2,1)} %reshape.123), calls=%async_computation.1 | async-start | bytes 4194304 | tf_op jit(solution)/shard_map/all_to_all | solution.py:51
  171.8 121.8 %reduce-scatter.4.cloned.1.call-start = ((), (), s32[]{:S(2)}) async-start(), calls=%async_computation.8 | async-start | bytes 3932160 | tf_op jit(solution)/shard_map/reduce_scatter | solution.py:88
  177.2 3.5 %copy-start.11 = (bf16[384,768]{1,0:T(8,128)(2,1)S(1)}, bf16[384,768]{1,0:T(8,128)(2,1)}, u32[]{:S(2)}) copy-start(bf16[384,768]{1,0:T(8,128)(2,1)} %copy-done.10) | copy-start | bytes 1769476
  221.5 1.3 copy-start.2
  222.8 56.8 %all-to-all-start.3 = ((bf16[64,6,2048]{2,1,0:T(8,128)(2,1)}), bf16[64,6,2048]{2,1,0:T(8,128)(2,1)}, u32[]{:S(2)}, u32[]{:S(2)}) async-start(bf16[64,6,2048]{2,1,0:T(8,128)(2,1)} %reshape.127), calls=%async_computation.3 | async-start | bytes 4194304 | tf_op jit(solution)/shard_map/all_to_all | solution.py:101
  234.0 2.3 copy-start.1
  283.6 6.1 %copy-start.3 = (f32[128,2,2048]{2,1,0:T(2,128)S(1)}, f32[128,2,2048]{2,1,0:T(2,128)}, u32[]{:S(2)}) copy-start(f32[128,2,2048]{2,1,0:T(2,128)} %reshape.129) | copy-start | bytes 6291460
Sparse Core Ops, SparseCore 0:
  10.6 98.0 all-gather.1
  155.5 38.5 reduce-scatter.7
  197.2 40.5 reduce-scatter.5
  240.8 40.5 reduce-scatter.3
where the time goes:
time: 302 us; the launch traced here: 300 us
  waiting for transfers between devices  158 us (52%)
  local copies, waits for them, and re-layouts  42.1 us (14%)
  matrix products  35.2 us (12%)
  starting transfers between devices  34.9 us (12%)
  other arithmetic  16.3 us (5%)
  between operations  14.1 us (5%)
    all_to_all x1, waiting for transfers between devices, shards(): lax.all_to_all(cot_slots.reshape(experts, capacity, model_width), 'expert...  45.8 us
    all_to_all x1, waiting for transfers between devices, shards(): lax.all_to_all(input_grad.reshape(experts, capacity, model_width), 'exper...  42.2 us
    all_to_all x1, waiting for transfers between devices, shards(): lax.all_to_all(outgoing.reshape(experts, capacity, model_width), 'expert'...  37 us
    all_to_all x1, waiting for transfers between devices, shards(): lax.all_to_all(expert_out.reshape(experts, capacity, model_width), 'exper...  32.5 us
    all_to_all x1, starting transfers between devices, shards(): lax.all_to_all(outgoing.reshape(experts, capacity, model_width), 'expert'...  13.3 us
    all_to_all x1, starting transfers between devices, shards(): lax.all_to_all(input_grad.reshape(experts, capacity, model_width), 'exper...  7.15 us
    all_to_all x1, starting transfers between devices, shards(): lax.all_to_all(expert_out.reshape(experts, capacity, model_width), 'exper...  6.97 us
    all_to_all x1, starting transfers between devices, shards(): lax.all_to_all(cot_slots.reshape(experts, capacity, model_width), 'expert...  6.96 us
  transfers between devices with their start and end apart: 8, of which 4 were waited for; matrix products, arithmetic and copies ran while one was open for 24% of the time, Pallas kernels for 0%

commit v1 on v0

v1 whole, which is shorter than its diff:
```python
import functools

import jax
import jax.numpy as jnp
import numpy as np
from jax import lax
from jax.experimental import pallas as pl
from jax.experimental.pallas import tpu as pltpu
from jax.sharding import PartitionSpec as P

MESH = pl.DeviceIdType.MESH
D, FF, TOK, CAP, NEXP, NDP = 2048, 768, 128, 6, 64, 4
SH = FF // NDP
HALF = SH // 2
SLOTS = NEXP * CAP
LANES = 512
PIECES = D // LANES
PEER = 2 * PIECES * CAP
GRP = 8
GROWS = GRP * PEER
GSLOTS = GRP * CAP
BF, F32, I32 = jnp.bfloat16, jnp.float32, jnp.int32
FCHUNK = 256

_r = np.arange(GROWS)
_peer, _kind, _piece, _slot = _r // PEER, _r % PEER // (PIECES * CAP), _r % (PIECES * CAP) // CAP, _r % CAP
BASE = (_peer * CAP + _slot).astype(np.int32)[:, None]
ISCOT = (_kind == 1).astype(np.float32)[:, None]
BLOCKMASK = np.repeat(
    (_kind * PIECES + _piece)[:, None] == np.arange(2 * PIECES)[None, :], TOK, axis=1
).astype(np.float32)
_dest = (_kind * PIECES + _piece) * GSLOTS + _peer * CAP + _slot
PERM = np.zeros((GROWS, GROWS), np.float32)
PERM[_dest, _r] = 1.0


def dot(a, b, ca=1, cb=0):
    return lax.dot_general(a, b, (((ca,), (cb,)), ((), ())), preferred_element_type=F32)


def place():
    me, y = lax.axis_index("expert"), lax.axis_index("dp")
    return me, y, me // 8, (me // 2) % 4, me % 2


def barrier(sems):
    me, y, z, x, c = place()
    at = lambda z, x, c: z * 8 + x * 2 + c
    zs = [at((z + 1) % 8, x, c), at((z + 7) % 8, x, c)]
    xs = [at(z, (x + 1) % 4, c), at(z, (x + 3) % 4, c)]
    cs = [at(z, x, 1 - c)]
    bar = pltpu.get_barrier_semaphore()

    def tell(sem, devices):
        for d in devices:
            pl.semaphore_signal(sem, inc=1, device_id=d, device_id_type=MESH)

    tell(bar, [(d, y) for d in zs + xs + cs] + [(me, (y + 1) % 4), (me, (y + 3) % 4)])
    pl.semaphore_wait(bar, 7)
    for i, group in enumerate((zs, zs, zs, xs, xs, cs)):
        tell(sems.at[i], [(d, y) for d in group])
        pl.semaphore_wait(sems.at[i], len(group))


def remote(src, dst, send, recv, device):
    return pltpu.make_async_remote_copy(src, dst, send, recv, device_id=device, device_id_type=MESH)


def start_exchange(src, dst, send, recv, local):
    me, y, z, x, c = place()
    own = pltpu.make_async_copy(src.at[me], dst.at[me], local)
    own.start()

    def one(k, carry):
        peer = ((z + k // 8) % 8) * 8 + ((x + (k // 2) % 4) % 4) * 2 + (c + k % 2) % 2
        remote(src.at[peer], dst.at[me], send, recv, (peer, y)).start()
        return carry

    lax.fori_loop(1, NEXP, one, 0)
    return own


def finish_exchange(src, dst, send, recv, own):
    n = NEXP - 1
    pltpu.make_async_copy(dst.at[pl.ds(0, n)], dst.at[pl.ds(0, n)], recv).wait()
    pltpu.make_async_copy(src.at[pl.ds(0, n)], src.at[pl.ds(0, n)], send).wait()
    own.wait()


def targets_row(ids, ids_t):
    before = lax.broadcasted_iota(I32, (TOK, TOK), 0) < lax.broadcasted_iota(I32, (TOK, TOK), 1)
    out = []
    for k in range(2):
        mine = ids_t[k : k + 1, :]
        same = (ids[:, 0:1] == mine).astype(F32) + (ids[:, 1:2] == mine).astype(F32)
        pos = jnp.sum(jnp.where(before, same, 0.0), axis=0, keepdims=True)
        out.append(mine * CAP + pos.astype(I32))
    return out


def targets_col(ids, ids_t):
    before = lax.broadcasted_iota(I32, (TOK, TOK), 1) < lax.broadcasted_iota(I32, (TOK, TOK), 0)
    out = []
    for k in range(2):
        mine = ids[:, k : k + 1]
        same = (ids_t[0:1, :] == mine).astype(F32) + (ids_t[1:2, :] == mine).astype(F32)
        pos = jnp.sum(jnp.where(before, same, 0.0), axis=1, keepdims=True)
        out.append(mine * CAP + pos.astype(I32))
    return out


def pack_kernel(tok, grad, ids, ids_t, sc_t, base, iscot, mask, out, table):
    for piece in range(PIECES):
        lanes = slice(piece * LANES, (piece + 1) * LANES)
        table[piece * TOK : (piece + 1) * TOK, :] = tok[:, lanes]
        table[(PIECES + piece) * TOK : (PIECES + piece + 1) * TOK, :] = grad[:, lanes]
    t0, t1 = targets_row(ids[...], ids_t[...])
    s0, s1 = sc_t[0:1, :], sc_t[1:2, :]

    def one(g, carry):
        slot = base[...] + g * GSLOTS
        h0, h1 = t0 == slot, t1 == slot
        score = jnp.sum(jnp.where(h0, s0, 0.0) + jnp.where(h1, s1, 0.0), axis=1, keepdims=True)
        scale = jnp.where(iscot[...] > 0.0, score, 1.0)
        hit = (h0.astype(F32) + h1.astype(F32)).astype(BF)
        pick = jnp.concatenate([hit] * (2 * PIECES), axis=1) * mask[...]
        rows = dot(pick, table[...]) * scale
        out[pl.ds(pl.multiple_of(g * GROWS, GROWS), GROWS), :] = rows.astype(BF)
        return carry

    lax.fori_loop(0, NEXP // GRP, one, 0)


def dispatch_kernel(x, wg, wu, wd, out, fg, fu, fd, bsem, xs, xr, loc, ws, wr):
    me, y, *_ = place()
    up, dn = (y + 1) % 4, (y + 3) % 4
    shards, fulls = (wg, wu, wd), (fg, fu, fd)
    at = lambda ref, who, off, n: ref.at[pl.ds(pl.multiple_of(who * SH + off, 32), n)]
    mine = [pltpu.make_async_copy(s, at(f, y, 0, SH), loc.at[1 + m]) for m, (s, f) in enumerate(zip(shards, fulls))]
    for q in mine:
        q.start()
    barrier(bsem)
    first, relay = [], []
    for m, (s, f) in enumerate(zip(shards, fulls)):
        for way, to in enumerate((up, dn)):
            q = remote(s, at(f, y, 0, SH), ws.at[way, m], wr.at[way, m], (me, to))
            q.start()
            first.append((m, way, q))
    own = start_exchange(x, out, xs, xr, loc.at[0])
    for m, way, q in first:
        q.wait_recv()
        part = at(fulls[m], dn if way == 0 else up, way * HALF, HALF)
        r = remote(part, part, ws.at[2 + way, m], wr.at[2 + way, m], (me, up if way == 0 else dn))
        r.start()
        relay.append(r)
    for q in relay:
        q.wait()
    for _, _, q in first:
        q.wait_send()
    for q in mine:
        q.wait()
    finish_exchange(x, out, xs, xr, own)


def unpack_rows(perm, rows, first, second):
    def one(g, carry):
        z = dot(perm[...], rows[pl.ds(pl.multiple_of(g * GROWS, GROWS), GROWS), :]).astype(BF)
        at = pl.ds(pl.multiple_of(g * GSLOTS, GSLOTS), GSLOTS)
        for kind, ref in enumerate((first, second)):
            for piece in range(PIECES):
                o = (kind * PIECES + piece) * GSLOTS
                ref[at, piece * LANES : (piece + 1) * LANES] = z[o : o + GSLOTS]
        return carry

    lax.fori_loop(0, NEXP // GRP, one, 0)


def pack_rows(perm, out, first, second):
    def one(g, carry):
        at = pl.ds(pl.multiple_of(g * GSLOTS, GSLOTS), GSLOTS)
        z = [
            ref[at, piece * LANES : (piece + 1) * LANES].astype(BF)
            for ref in (first, second)
            for piece in range(PIECES)
        ]
        packed = dot(perm[...], jnp.concatenate(z, axis=0), 0, 0)
        out[pl.ds(pl.multiple_of(g * GROWS, GROWS), GROWS), :] = packed.astype(BF)
        return carry

    lax.fori_loop(0, NEXP // GRP, one, 0)


def expert_kernel(rows, perm, wg, wu, wd, out, dg, du, dd, xt, xc, acc_o, acc_i):
    step = pl.program_id(0)

    @pl.when(step == 0)
    def _():
        unpack_rows(perm, rows, xt, xc)

    gate = dot(xt[...], wg[...], 1, 1)
    up = dot(xt[...], wu[...], 1, 1)
    hg = dot(xc[...], wd[...], 1, 1)
    s = jax.nn.sigmoid(gate)
    act = gate * s
    hidden = (act * up).astype(BF)
    ggrad = (hg * up * (s * (1.0 + gate * (1.0 - s)))).astype(BF)
    ugrad = (hg * act).astype(BF)
    dg[...] = dot(ggrad, xt[...], 0, 0).astype(BF)
    du[...] = dot(ugrad, xt[...], 0, 0).astype(BF)
    dd[...] = dot(hidden, xc[...], 0, 0).astype(BF)
    o = dot(hidden, wd[...])
    i = dot(ggrad, wg[...]) + dot(ugrad, wu[...])

    @pl.when(step == 0)
    def _():
        acc_o[...] = o
        acc_i[...] = i

    @pl.when(step > 0)
    def _():
        acc_o[...] += o
        acc_i[...] += i

    @pl.when(step == FF // FCHUNK - 1)
    def _():
        pack_rows(perm, out, acc_o, acc_i)


def return_kernel(
    x, pg, pu, pd, out, og, ou, od, bsem, xs, xr, loc, rel, add, summed, frm, own_w, rs_s, rs_r
):
    me, y, *_ = place()
    up, dn, far = (y + 1) % 4, (y + 3) % 4, (y + 2) % 4
    parts = (pg, pu, pd)
    at = lambda ref, who, off, n: ref.at[pl.ds(pl.multiple_of(who * SH + off, 32), n)]
    loads = []
    for m, p in enumerate(parts):
        qs = [
            pltpu.make_async_copy(at(p, up, 0, HALF), add.at[0, m], loc.at[1 + m]),
            pltpu.make_async_copy(at(p, dn, HALF, HALF), add.at[1, m], loc.at[4 + m]),
            pltpu.make_async_copy(at(p, y, 0, SH), own_w.at[m], loc.at[7 + m]),
        ]
        for q in qs:
            q.start()
        loads.append(qs)
    barrier(bsem)
    tos = (up, dn)
    relays, directs, sums = [], [], []
    for m, p in enumerate(parts):
        for way in range(2):
            q = remote(at(p, far, way * HALF, HALF), rel.at[way, m], rs_s.at[way, m], rs_r.at[way, m], (me, tos[way]))
            q.start()
            relays.append((m, way, q))
    for m, p in enumerate(parts):
        for way in range(2):
            off = (1 - way) * HALF
            q = remote(
                at(p, tos[way], off, HALF),
                frm.at[way, m, pl.ds(off, HALF)],
                rs_s.at[2 + way, m],
                rs_r.at[2 + way, m],
                (me, tos[way]),
            )
            q.start()
            directs.append(q)
    own = start_exchange(x, out, xs, xr, loc.at[0])
    for m, way, q in relays:
        q.wait_recv()
        loads[m][way].wait()

        def add_rows(r, carry):
            rows = pl.ds(pl.multiple_of(r * 32, 32), 32)
            total = rel[way, m, rows, :].astype(F32) + add[way, m, rows, :].astype(F32)
            summed[way, m, rows, :] = total.astype(BF)
            return carry

        lax.fori_loop(0, HALF // 32, add_rows, 0)
        off = way * HALF
        s = remote(
            summed.at[way, m], frm.at[way, m, pl.ds(off, HALF)], rs_s.at[4 + way, m], rs_r.at[4 + way, m], (me, tos[way])
        )
        s.start()
        sums.append(s)
    for q in directs:
        q.wait()
    for q in sums:
        q.wait()
    for m, (_, ref) in enumerate(zip(parts, (og, ou, od))):
        loads[m][2].wait()

        def final(r, carry):
            rows = pl.ds(pl.multiple_of(r * 32, 32), 32)
            total = own_w[m, rows, :].astype(F32) + frm[0, m, rows, :].astype(F32)
            ref[rows, :] = (total + frm[1, m, rows, :].astype(F32)).astype(BF)
            return carry

        lax.fori_loop(0, SH // 32, final, 0)
    for _, _, q in relays:
        q.wait_send()
    finish_exchange(x, out, xs, xr, own)


def combine_kernel(rows, perm, grad, ids, ids_t, sc, out, dtok, dsc, xo, xi):
    unpack_rows(perm, rows, xo, xi)
    t0, t1 = targets_col(ids[...], ids_t[...])
    slot = lax.broadcasted_iota(I32, (TOK, SLOTS), 1)
    g0 = (t0 == slot).astype(F32).astype(BF)
    g1 = (t1 == slot).astype(F32).astype(BF)
    both = g0 + g1
    s0, s1 = sc[:, 0:1], sc[:, 1:2]
    d0 = jnp.zeros((TOK, 1), F32)
    d1 = jnp.zeros((TOK, 1), F32)
    for piece in range(PIECES):
        lanes = slice(piece * LANES, (piece + 1) * LANES)
        p0 = dot(g0, xo[:, lanes])
        p1 = dot(g1, xo[:, lanes])
        og = grad[:, lanes].astype(F32)
        out[:, lanes] = (s0 * p0 + s1 * p1).astype(BF)
        d0 += jnp.sum(og * p0, axis=1, keepdims=True)
        d1 += jnp.sum(og * p1, axis=1, keepdims=True)
        dtok[:, lanes] = dot(both, xi[:, lanes]).astype(BF)
    dsc[...] = jnp.concatenate([d0, d1], axis=1)


def shards(tokens, expert_ids, gate_scores, gate_proj, up_proj, down_proj, out_grad):
    sd = jax.ShapeDtypeStruct
    vm = pl.BlockSpec(memory_space=pltpu.VMEM)
    anyw = pl.BlockSpec(memory_space=pl.ANY)
    dma, reg = pltpu.SemaphoreType.DMA, pltpu.SemaphoreType.REGULAR
    ids_t, sc_t = expert_ids.T, gate_scores.T
    perm = jnp.asarray(PERM, BF)
    big = NEXP * PEER
    packed = pl.pallas_call(
        pack_kernel,
        name="pack",
        out_shape=sd((big, LANES), BF),
        in_specs=[vm] * 8,
        out_specs=vm,
        scratch_shapes=[pltpu.VMEM((2 * PIECES * TOK, LANES), BF)],
        compiler_params=pltpu.CompilerParams(vmem_limit_bytes=48 << 20),
    )(tokens, out_grad, expert_ids, ids_t, sc_t, jnp.asarray(BASE), jnp.asarray(ISCOT), jnp.asarray(BLOCKMASK, BF))
    wg, wu, wd = gate_proj[0], up_proj[0], down_proj[0]
    received, fg, fu, fd = pl.pallas_call(
        dispatch_kernel,
        name="dispatch",
        out_shape=(sd((NEXP, PEER, LANES), BF),) + (sd((FF, D), BF),) * 3,
        in_specs=[anyw] * 4,
        out_specs=(anyw,) * 4,
        scratch_shapes=[reg((6,)), dma, dma, dma((4,)), dma((4, 3)), dma((4, 3))],
        compiler_params=pltpu.CompilerParams(collective_id=1, has_side_effects=True, vmem_limit_bytes=16 << 20),
    )(packed.reshape(NEXP, PEER, LANES), wg, wu, wd)
    wspec = pl.BlockSpec((FCHUNK, D), lambda i: (i, 0))
    whole = lambda *shape: pl.BlockSpec(shape, lambda i: (0, 0))
    back, pg, pu, pd = pl.pallas_call(
        expert_kernel,
        name="expert",
        grid=(FF // FCHUNK,),
        out_shape=(sd((big, LANES), BF),) + (sd((FF, D), BF),) * 3,
        in_specs=[whole(big, LANES), whole(GROWS, GROWS)] + [wspec] * 3,
        out_specs=(whole(big, LANES),) + (wspec,) * 3,
        scratch_shapes=[pltpu.VMEM((SLOTS, D), BF)] * 2 + [pltpu.VMEM((SLOTS, D), F32)] * 2,
        compiler_params=pltpu.CompilerParams(vmem_limit_bytes=60 << 20),
    )(received.reshape(big, LANES), perm, fg, fu, fd)
    returned, gg, gu, gd = pl.pallas_call(
        return_kernel,
        name="giveback",
        out_shape=(sd((NEXP, PEER, LANES), BF),) + (sd((SH, D), BF),) * 3,
        in_specs=[anyw] * 4,
        out_specs=(anyw, vm, vm, vm),
        scratch_shapes=[
            reg((6,)),
            dma,
            dma,
            dma((10,)),
            pltpu.VMEM((2, 3, HALF, D), BF),
            pltpu.VMEM((2, 3, HALF, D), BF),
            pltpu.VMEM((2, 3, HALF, D), BF),
            pltpu.VMEM((2, 3, SH, D), BF),
            pltpu.VMEM((3, SH, D), BF),
            dma((6, 3)),
            dma((6, 3)),
        ],
        compiler_params=pltpu.CompilerParams(collective_id=2, has_side_effects=True, vmem_limit_bytes=48 << 20),
    )(back.reshape(NEXP, PEER, LANES), pg, pu, pd)
    output, d_tokens, d_scores = pl.pallas_call(
        combine_kernel,
        name="combine",
        out_shape=(sd((TOK, D), BF), sd((TOK, D), BF), sd((TOK, 2), F32)),
        in_specs=[vm] * 6,
        out_specs=(vm,) * 3,
        scratch_shapes=[pltpu.VMEM((SLOTS, D), BF)] * 2,
        compiler_params=pltpu.CompilerParams(vmem_limit_bytes=48 << 20),
    )(returned.reshape(big, LANES), perm, out_grad, expert_ids, ids_t, gate_scores)
    return output, d_tokens, d_scores, gg[None], gu[None], gd[None]


def solution(mesh):
    rows, weights = P(("expert", "dp"), None), P("expert", "dp", None)
    return jax.shard_map(
        shards,
        mesh=mesh,
        in_specs=(rows, rows, rows, weights, weights, weights, rows),
        out_specs=(rows, rows, rows, weights, weights, weights),
        check_vma=False,
    )
```

time: 302 us -> 254 us (0.84)
  Pallas kernels: 0 us -> 227 us
  waiting for transfers between devices: 158 us -> 0 us
  matrix products: 35.2 us -> 0 us
  starting transfers between devices: 34.9 us -> 0 us
  other arithmetic: 16.3 us -> 0 us
  local copies, waits for them, and re-layouts: 42.1 us -> 26.4 us
  between operations: 14.1 us -> 0.74 us
    pallas_call x0 -> x5, Pallas kernels: none -> 227 us  [the longest x1 96.9 us: shards(): pl.pallas_call(dispatch_kernel, name='dispatch', out_shape=(sd((NEXP, PEE...]
    all_to_all x4 -> x0, waiting for transfers between devices: 157 us -> none  [the longest x1 45.8 us: shards(): lax.all_to_all(cot_slots.reshape(experts, capacity, model_width), 'expert...]
    dot_general x9 -> x0, matrix products: 35.2 us -> none  [the longest x1 5.13 us: shards(): jnp.dot(gate_grad.T, received, preferred_element_type=jnp.float32)[None]]
    all_to_all x4 -> x0, starting transfers between devices: 34.4 us -> none  [the longest x1 13.3 us: shards(): lax.all_to_all(outgoing.reshape(experts, capacity, model_width), 'expert'...]
    unnamed x31 -> x54, local copies, waits for them, and re-layouts: 4.71 us -> 26.4 us
    reshape x9 -> x0, local copies, waits for them, and re-layouts: 21.5 us -> none  [the longest x1 3.73 us: shards(): input_grad.reshape(experts, capacity, model_width)]
    reduce_sum x4 -> x0, other arithmetic: 8.87 us -> none  [the longest x1 4.57 us: shards(): jnp.sum(pair_input.reshape(tok_count, routes_per, model_width), axis=1)]
    convert_element_type x2 -> x0, local copies, waits for them, and re-layouts: 5 us -> none  [the longest x1 2.69 us: shards(): pair_grad = jnp.repeat(out_grad, routes_per, axis=0).astype(jnp.float32)]
  transfers between devices with their start and end apart: 8 -> 0, of which waited for: 4 -> 0; matrix products, arithmetic and copies ran while one was open for 24% -> 0% of each run, Pallas kernels for 0% -> 0%
where the time goes in v1:
time: 254 us
  Pallas kernels  227 us (89%)
  local copies, waits for them, and re-layouts  26.4 us (10%)
    pallas_call x1, Pallas kernels, shards(): pl.pallas_call(dispatch_kernel, name='dispatch', out_shape=(sd((NEXP, PEE...  96.9 us
    pallas_call x1, Pallas kernels, shards(): pl.pallas_call(return_kernel, name='giveback', out_shape=(sd((NEXP, PEER,...  89.8 us
    pallas_call x1, Pallas kernels, shards(): pl.pallas_call(expert_kernel, name='expert', grid=(FF // FCHUNK,), out_sh...  29.7 us
    unnamed x54, local copies, waits for them, and re-layouts  26.4 us
    pallas_call x1, Pallas kernels, shards(): pl.pallas_call(combine_kernel, name='combine', out_shape=(sd((TOK, D), BF...  5.2 us
    pallas_call x1, Pallas kernels, shards(): pl.pallas_call(pack_kernel, name='pack', out_shape=sd((big, LANES), BF),...  5.09 us

profile of v1, /device:TPU:1, one launch (start us, length us, event | category | flops | bytes accessed | tf_op | source)
XLA Modules:
  0.0 253.8 jit_solution(6391788094391746244)
XLA Ops:
  0.6 0.8 copy.17.ids
  1.4 1.0 copy-done.4
  2.5 1.1 copy-done.7
  3.6 1.0 copy-done.15
  4.6 0.9 copy-done.17
  5.6 0.9 copy-done.18
  6.5 0.7 copy-done.20
  7.2 0.7 copy-done.22
  7.9 5.1 %pack.1 = bf16[3072,512]{1,0:T(8,128)(2,1)S(1)} custom-call(bf16[128,2048]{1,0:T(8,128)(2,1)S(1)} %copy-done.15, bf16[128,2048]{1,0:T(8,128)(2,1)S(1)} %copy-done.4, s32[128,2]{1,0:T(8,128)S(1)} %copy.17.ids, s32[2,128]{1,0:T(2,128)S(1)} %bitcast.21, f32[2,128]{1,0:T(2,128)S(1)} %bitcast.23, s32[384,1]{1,0:T(8,128)S(1)} %copy-done.18, ...), custom_call_target="tpu_custom_call" | custom-call | tf_op jit(solution)/shard_map/pack/pallas_call | solution.py:333
  13.0 0.0 copy-done.12
  13.0 96.9 %dispatch.1 = (bf16[64,48,512]{2,1,0:T(8,128)(2,1)S(1)}, bf16[768,2048]{1,0:T(8,128)(2,1)S(1)}, bf16[768,2048]{1,0:T(8,128)(2,1)S(1)}, bf16[768,2048]{1,0:T(8,128)(2,1)S(1)}) custom-call(bf16[64,48,512]{2,1,0:T(8,128)(2,1)S(1)} %bitcast.12, bf16[192,2048]{1,0:T(8,128)(2,1)S(1)} %bitcast.18, bf16[192,2048]{1,0:T(8,128)(2,1)S(1)} %bitcast.19, ...), custom_call_target="tpu_custom_call" | custom-call | tf_op jit(solution)/shard_map/dispatch/pallas_call | solution.py:343
  109.9 0.0 copy-start
  109.9 1.6 copy-done
  111.5 1.7 copy-done.1
  113.2 1.7 copy-done.2
  114.9 1.7 copy-done.3
  116.6 29.7 %expert.1 = (bf16[3072,512]{1,0:T(8,128)(2,1)}, bf16[768,2048]{1,0:T(8,128)(2,1)}, bf16[768,2048]{1,0:T(8,128)(2,1)}, bf16[768,2048]{1,0:T(8,128)(2,1)}) custom-call(bf16[3072,512]{1,0:T(8,128)(2,1)} %bitcast.14, bf16[384,384]{1,0:T(8,128)(2,1)} %constant.8.clone.perm, bf16[768,2048]{1,0:T(8,128)(2,1)} %copy-done.1, bf16[768,2048]{1,0:T(8,128)(2,1)} %copy-done.2, ...), custom_call_target="tpu_custom_call" | custom-call | tf_op jit(solution)/shard_map/expert/pallas_call | solution.py:354
  146.2 0.0 copy-start.21
  146.3 89.8 %giveback.1 = (bf16[64,48,512]{2,1,0:T(8,128)(2,1)S(1)}, bf16[192,2048]{1,0:T(8,128)(2,1)S(1)}, bf16[192,2048]{1,0:T(8,128)(2,1)S(1)}, bf16[192,2048]{1,0:T(8,128)(2,1)S(1)}) custom-call(bf16[64,48,512]{2,1,0:T(8,128)(2,1)} %bitcast.24, bf16[768,2048]{1,0:T(8,128)(2,1)} %get-tuple-element.26.pg, bf16[768,2048]{1,0:T(8,128)(2,1)} %get-tuple-element.27.pu, ...), custom_call_target="tpu_custom_call" | custom-call | tf_op jit(solution)/shard_map/giveback/pallas_call | solution.py:364
  236.1 0.0 copy-start.8
  236.1 0.9 copy-done.8
  237.0 0.9 copy-done.10
  237.9 0.9 copy-done.11
  238.8 0.7 copy.19.sc
  239.5 1.0 copy-done.5
  240.6 0.8 copy-done.16
  241.4 5.2 %combine.1 = (bf16[128,2048]{1,0:T(8,128)(2,1)}, bf16[128,2048]{1,0:T(8,128)(2,1)}, f32[128,2]{1,0:T(8,128)S(1)}) custom-call(bf16[3072,512]{1,0:T(8,128)(2,1)S(1)} %bitcast.13, bf16[384,384]{1,0:T(8,128)(2,1)S(1)} %copy-done.6, bf16[128,2048]{1,0:T(8,128)(2,1)S(1)} %copy-done.5, s32[128,2]{1,0:T(8,128)S(1)} %copy.17.ids, s32[2,128]{1,0:T(2,128)S(1)} %bitcast.22, ...), custom_call_target="tpu_custom_call" | custom-call | tf_op jit(solution)/shard_map/combine/pallas_call | solution.py:385
  246.6 0.6 copy-done.19
  247.2 1.5 copy.20
  248.8 2.1 copy.24
  250.9 2.1 copy.25
  253.0 0.9 copy.26
  (27 shorter events, 0.0 us)
Async XLA Ops:
  1.4 1.0 copy-start.4
  2.5 1.1 copy-start.7
  3.6 1.0 copy-start.15
  4.6 0.9 copy-start.17
  5.6 0.9 copy-start.18
  6.5 0.7 copy-start.20
  7.2 0.7 copy-start.22
  7.8 5.1 %copy-start.12 = (bf16[1,192,2048]{2,1,0:T(8,128)(2,1)S(1)}, bf16[1,192,2048]{2,1,0:T(8,128)(2,1)}, u32[]{:S(2)}) copy-start(bf16[1,192,2048]{2,1,0:T(8,128)(2,1)} %param.14) | copy-start | bytes 2359300
  7.9 5.1 %copy-start.13 = (bf16[1,192,2048]{2,1,0:T(8,128)(2,1)S(1)}, bf16[1,192,2048]{2,1,0:T(8,128)(2,1)}, u32[]{:S(2)}) copy-start(bf16[1,192,2048]{2,1,0:T(8,128)(2,1)} %param.15) | copy-start | bytes 2359300
  7.9 5.1 %copy-start.14 = (bf16[1,192,2048]{2,1,0:T(8,128)(2,1)S(1)}, bf16[1,192,2048]{2,1,0:T(8,128)(2,1)}, u32[]{:S(2)}) copy-start(bf16[1,192,2048]{2,1,0:T(8,128)(2,1)} %param.16) | copy-start | bytes 2359300
  109.9 1.6 copy-start
  111.5 1.7 copy-start.1
  113.2 1.7 copy-start.2
  114.9 1.7 copy-start.3
  146.2 92.5 %copy-start.23 = (f32[128,2]{0,1:T(2,128)S(1)}, f32[128,2]{0,1:T(2,128)}, u32[]{:S(2)}) copy-start(f32[128,2]{0,1:T(2,128)} %param.13) | copy-start | bytes 3076
  146.2 93.3 %copy-start.6 = (bf16[384,384]{1,0:T(8,128)(2,1)S(1)}, bf16[384,384]{1,0:T(8,128)(2,1)}, u32[]{:S(2)}) copy-start(bf16[384,384]{1,0:T(8,128)(2,1)} %constant.8.clone.perm) | copy-start | bytes 884740
  146.2 93.3 %copy-start.21 = (s32[128,2]{0,1:T(2,128)S(1)}, s32[128,2]{0,1:T(2,128)}, u32[]{:S(2)}) copy-start(s32[128,2]{0,1:T(2,128)} %param.12) | copy-start | bytes 3076
  236.1 0.9 copy-start.8
  237.0 0.9 copy-start.10
  237.9 0.9 copy-start.11
  239.5 1.0 copy-start.5
  240.6 0.8 copy-start.16
  246.6 0.6 copy-start.19
  247.2 5.7 %copy-start.9 = (bf16[192,2048]{1,0:T(8,128)(2,1)S(1)}, bf16[192,2048]{1,0:T(8,128)(2,1)}, u32[]{:S(2)}) copy-start(bf16[192,2048]{1,0:T(8,128)(2,1)} %copy-done.8) | copy-start | bytes 2359300

commit v2 on v1

--- a/solution.py
+++ b/solution.py
@@ -24,11 +24,6 @@
 
 _r = np.arange(GROWS)
 _peer, _kind, _piece, _slot = _r // PEER, _r % PEER // (PIECES * CAP), _r % (PIECES * CAP) // CAP, _r % CAP
-BASE = (_peer * CAP + _slot).astype(np.int32)[:, None]
-ISCOT = (_kind == 1).astype(np.float32)[:, None]
-BLOCKMASK = np.repeat(
-    (_kind * PIECES + _piece)[:, None] == np.arange(2 * PIECES)[None, :], TOK, axis=1
-).astype(np.float32)
 _dest = (_kind * PIECES + _piece) * GSLOTS + _peer * CAP + _slot
 PERM = np.zeros((GROWS, GROWS), np.float32)
 PERM[_dest, _r] = 1.0
@@ -43,22 +38,26 @@
     return me, y, me // 8, (me // 2) % 4, me % 2
 
 
-def barrier(sems):
+def tell(sem, devices):
+    for d in devices:
+        pl.semaphore_signal(sem, inc=1, device_id=d, device_id_type=MESH)
+
+
+def barrier(sems, greeted=None, between=None):
     me, y, z, x, c = place()
     at = lambda z, x, c: z * 8 + x * 2 + c
     zs = [at((z + 1) % 8, x, c), at((z + 7) % 8, x, c)]
     xs = [at(z, (x + 1) % 4, c), at(z, (x + 3) % 4, c)]
     cs = [at(z, x, 1 - c)]
     bar = pltpu.get_barrier_semaphore()
-
-    def tell(sem, devices):
-        for d in devices:
-            pl.semaphore_signal(sem, inc=1, device_id=d, device_id_type=MESH)
-
     tell(bar, [(d, y) for d in zs + xs + cs] + [(me, (y + 1) % 4), (me, (y + 3) % 4)])
     pl.semaphore_wait(bar, 7)
+    if greeted is not None:
+        greeted()
     for i, group in enumerate((zs, zs, zs, xs, xs, cs)):
         tell(sems.at[i], [(d, y) for d in group])
+        if between is not None:
+            between(i)
         pl.semaphore_wait(sems.at[i], len(group))
 
 
@@ -94,7 +93,7 @@
         mine = ids_t[k : k + 1, :]
         same = (ids[:, 0:1] == mine).astype(F32) + (ids[:, 1:2] == mine).astype(F32)
         pos = jnp.sum(jnp.where(before, same, 0.0), axis=0, keepdims=True)
-        out.append(mine * CAP + pos.astype(I32))
+        out.append(mine * CAP + pos)
     return out
 
 
@@ -105,47 +104,66 @@
         mine = ids[:, k : k + 1]
         same = (ids_t[0:1, :] == mine).astype(F32) + (ids_t[1:2, :] == mine).astype(F32)
         pos = jnp.sum(jnp.where(before, same, 0.0), axis=1, keepdims=True)
-        out.append(mine * CAP + pos.astype(I32))
+        out.append(mine * CAP + pos)
     return out
 
 
-def pack_kernel(tok, grad, ids, ids_t, sc_t, base, iscot, mask, out, table):
-    for piece in range(PIECES):
-        lanes = slice(piece * LANES, (piece + 1) * LANES)
-        table[piece * TOK : (piece + 1) * TOK, :] = tok[:, lanes]
-        table[(PIECES + piece) * TOK : (PIECES + piece + 1) * TOK, :] = grad[:, lanes]
-    t0, t1 = targets_row(ids[...], ids_t[...])
+def columns(pair):
+    return jnp.concatenate([pair] * 4, axis=0).T
+
+
+def pack_group(g, ids_t, ids, sc_t, out, table):
+    t0, t1 = targets_row(ids, ids_t)
     s0, s1 = sc_t[0:1, :], sc_t[1:2, :]
-
-    def one(g, carry):
-        slot = base[...] + g * GSLOTS
-        h0, h1 = t0 == slot, t1 == slot
-        score = jnp.sum(jnp.where(h0, s0, 0.0) + jnp.where(h1, s1, 0.0), axis=1, keepdims=True)
-        scale = jnp.where(iscot[...] > 0.0, score, 1.0)
-        hit = (h0.astype(F32) + h1.astype(F32)).astype(BF)
-        pick = jnp.concatenate([hit] * (2 * PIECES), axis=1) * mask[...]
-        rows = dot(pick, table[...]) * scale
-        out[pl.ds(pl.multiple_of(g * GROWS, GROWS), GROWS), :] = rows.astype(BF)
-        return carry
-
-    lax.fori_loop(0, NEXP // GRP, one, 0)
-
-
-def dispatch_kernel(x, wg, wu, wd, out, fg, fu, fd, bsem, xs, xr, loc, ws, wr):
+    row = lax.broadcasted_iota(I32, (GROWS, 1), 0).astype(F32)
+    six = jnp.floor((row + 0.5) * (1.0 / CAP))
+    peer = jnp.floor((six + 0.5) * (1.0 / (2 * PIECES)))
+    block = six - 2 * PIECES * peer
+    slot = peer * CAP + (row - CAP * six) + float(g * GSLOTS)
+    h0, h1 = t0 == slot, t1 == slot
+    score = jnp.sum(jnp.where(h0, s0, 0.0) + jnp.where(h1, s1, 0.0), axis=1, keepdims=True)
+    scale = jnp.where(block > PIECES - 0.5, score, 1.0)
+    hit = h0.astype(F32) + h1.astype(F32)
+    pick = jnp.concatenate([jnp.where(block == float(b), hit, 0.0).astype(BF) for b in range(2 * PIECES)], axis=1)
+    rows = dot(pick, table[...]) * scale
+    out[g * GRP : (g + 1) * GRP] = rows.astype(BF).reshape(GRP, PEER, LANES)
+
+
+def dispatch_kernel(
+    tok, grad, ids, sc, wg, wu, wd, out, fg, fu, fd, bsem, xs, xr, loc, ws, wr, tv, gv, iv, sv, table, x
+):
     me, y, *_ = place()
     up, dn = (y + 1) % 4, (y + 3) % 4
     shards, fulls = (wg, wu, wd), (fg, fu, fd)
     at = lambda ref, who, off, n: ref.at[pl.ds(pl.multiple_of(who * SH + off, 32), n)]
+    loads = [
+        pltpu.make_async_copy(s, d, loc.at[4 + i]) for i, (s, d) in enumerate(((ids, iv), (sc, sv), (tok, tv), (grad, gv)))
+    ]
     mine = [pltpu.make_async_copy(s, at(f, y, 0, SH), loc.at[1 + m]) for m, (s, f) in enumerate(zip(shards, fulls))]
-    for q in mine:
+    for q in loads + mine:
         q.start()
-    barrier(bsem)
     first, relay = [], []
-    for m, (s, f) in enumerate(zip(shards, fulls)):
-        for way, to in enumerate((up, dn)):
-            q = remote(s, at(f, y, 0, SH), ws.at[way, m], wr.at[way, m], (me, to))
-            q.start()
-            first.append((m, way, q))
+
+    def gather():
+        for m, (s, f) in enumerate(zip(shards, fulls)):
+            for way, to in enumerate((up, dn)):
+                q = remote(s, at(f, y, 0, SH), ws.at[way, m], wr.at[way, m], (me, to))
+                q.start()
+                first.append((m, way, q))
+
+    def pack(i):
+        if i == 0:
+            for q in loads:
+                q.wait()
+            for piece in range(PIECES):
+                lanes = slice(piece * LANES, (piece + 1) * LANES)
+                table[piece * TOK : (piece + 1) * TOK, :] = tv[:, lanes]
+                table[(PIECES + piece) * TOK : (PIECES + piece + 1) * TOK, :] = gv[:, lanes]
+        ids_t = iv[...].astype(F32)
+        for g in ((0,), (1, 2), (3, 4), (5, 6), (7,), ())[i]:
+            pack_group(g, ids_t, columns(ids_t), sv[...], x, table)
+
+    barrier(bsem, gather, pack)
     own = start_exchange(x, out, xs, xr, loc.at[0])
     for m, way, q in first:
         q.wait_recv()
@@ -162,7 +180,7 @@
     finish_exchange(x, out, xs, xr, own)
 
 
-def unpack_rows(perm, rows, first, second):
+def unpack_rows(perm, rows, first, second, start=0, stop=NEXP // GRP):
     def one(g, carry):
         z = dot(perm[...], rows[pl.ds(pl.multiple_of(g * GROWS, GROWS), GROWS), :]).astype(BF)
         at = pl.ds(pl.multiple_of(g * GSLOTS, GSLOTS), GSLOTS)
@@ -172,7 +190,7 @@
                 ref[at, piece * LANES : (piece + 1) * LANES] = z[o : o + GSLOTS]
         return carry
 
-    lax.fori_loop(0, NEXP // GRP, one, 0)
+    lax.fori_loop(start, stop, one, 0)
 
 
 def pack_rows(perm, out, first, second):
@@ -227,7 +245,7 @@
 
 
 def return_kernel(
-    x, pg, pu, pd, out, og, ou, od, bsem, xs, xr, loc, rel, add, summed, frm, own_w, rs_s, rs_r
+    x, pg, pu, pd, out, frm, bsem, xs, xr, loc, rel, add, summed, rs_s, rs_r
 ):
     me, y, *_ = place()
     up, dn, far = (y + 1) % 4, (y + 3) % 4, (y + 2) % 4
@@ -238,7 +256,6 @@
         qs = [
             pltpu.make_async_copy(at(p, up, 0, HALF), add.at[0, m], loc.at[1 + m]),
             pltpu.make_async_copy(at(p, dn, HALF, HALF), add.at[1, m], loc.at[4 + m]),
-            pltpu.make_async_copy(at(p, y, 0, SH), own_w.at[m], loc.at[7 + m]),
         ]
         for q in qs:
             q.start()
@@ -285,41 +302,76 @@
         q.wait()
     for q in sums:
         q.wait()
-    for m, (_, ref) in enumerate(zip(parts, (og, ou, od))):
-        loads[m][2].wait()
-
-        def final(r, carry):
-            rows = pl.ds(pl.multiple_of(r * 32, 32), 32)
-            total = own_w[m, rows, :].astype(F32) + frm[0, m, rows, :].astype(F32)
-            ref[rows, :] = (total + frm[1, m, rows, :].astype(F32)).astype(BF)
-            return carry
-
-        lax.fori_loop(0, SH // 32, final, 0)
     for _, _, q in relays:
         q.wait_send()
     finish_exchange(x, out, xs, xr, own)
 
 
-def combine_kernel(rows, perm, grad, ids, ids_t, sc, out, dtok, dsc, xo, xi):
-    unpack_rows(perm, rows, xo, xi)
-    t0, t1 = targets_col(ids[...], ids_t[...])
-    slot = lax.broadcasted_iota(I32, (TOK, SLOTS), 1)
+def combine_kernel(
+    rows_h, frm_h, perm_h, grad_h, ids_h, sc_h, pg, pu, pd,
+    out, dtok, dsc, og, ou, od,
+    rows, frm, perm, grad, ids, sc, xo, xi, own, fin, sem, rsem,
+):
+    y = lax.axis_index("dp")
+    parts, outs = (pg, pu, pd), (og, ou, od)
+    small = [
+        pltpu.make_async_copy(s, d, sem.at[6 + i])
+        for i, (s, d) in enumerate(((perm_h, perm), (grad_h, grad), (ids_h, ids), (sc_h, sc)))
+    ]
+    span = 2 * GROWS
+    chunks = [
+        pltpu.make_async_copy(rows_h.at[pl.ds(i * span, span)], rows.at[pl.ds(i * span, span)], rsem.at[i]) for i in range(4)
+    ]
+    load = [
+        [
+            pltpu.make_async_copy(p.at[pl.ds(pl.multiple_of(y * SH, 32), SH)], own.at[m], sem.at[m]),
+            pltpu.make_async_copy(frm_h.at[0, m], frm.at[0, m], sem.at[10 + m]),
+            pltpu.make_async_copy(frm_h.at[1, m], frm.at[1, m], sem.at[13 + m]),
+        ]
+        for m, p in enumerate(parts)
+    ]
+    store = [pltpu.make_async_copy(fin.at[m], o, sem.at[3 + m]) for m, o in enumerate(outs)]
+    for q in small + chunks + sum(load, []):
+        q.start()
+    for q in small:
+        q.wait()
+    for i in range(4):
+        chunks[i].wait()
+        unpack_rows(perm, rows, xo, xi, 2 * i, 2 * i + 2)
+    for m in range(3):
+        for q in load[m]:
+            q.wait()
+
+        def final(r, carry):
+            at = pl.ds(pl.multiple_of(r * 32, 32), 32)
+            total = own[m, at, :].astype(F32) + frm[0, m, at, :].astype(F32)
+            fin[m, at, :] = (total + frm[1, m, at, :].astype(F32)).astype(BF)
+            return carry
+
+        lax.fori_loop(0, SH // 32, final, 0)
+        store[m].start()
+    ids_t = ids[...].astype(F32)
+    t0, t1 = targets_col(columns(ids_t), ids_t)
+    slot = lax.broadcasted_iota(I32, (TOK, SLOTS), 1).astype(F32)
     g0 = (t0 == slot).astype(F32).astype(BF)
     g1 = (t1 == slot).astype(F32).astype(BF)
     both = g0 + g1
-    s0, s1 = sc[:, 0:1], sc[:, 1:2]
+    sc_c = columns(sc[...])
+    s0, s1 = sc_c[:, 0:1], sc_c[:, 1:2]
     d0 = jnp.zeros((TOK, 1), F32)
     d1 = jnp.zeros((TOK, 1), F32)
     for piece in range(PIECES):
         lanes = slice(piece * LANES, (piece + 1) * LANES)
         p0 = dot(g0, xo[:, lanes])
         p1 = dot(g1, xo[:, lanes])
-        og = grad[:, lanes].astype(F32)
+        cot = grad[:, lanes].astype(F32)
         out[:, lanes] = (s0 * p0 + s1 * p1).astype(BF)
-        d0 += jnp.sum(og * p0, axis=1, keepdims=True)
-        d1 += jnp.sum(og * p1, axis=1, keepdims=True)
+        d0 += jnp.sum(cot * p0, axis=1, keepdims=True)
+        d1 += jnp.sum(cot * p1, axis=1, keepdims=True)
         dtok[:, lanes] = dot(both, xi[:, lanes]).astype(BF)
-    dsc[...] = jnp.concatenate([d0, d1], axis=1)
+    dsc[...] = jnp.concatenate([d0, d1] * 4, axis=1).T[0:2, :]
+    for q in store:
+        q.wait()
 
 
 def shards(tokens, expert_ids, gate_scores, gate_proj, up_proj, down_proj, out_grad):
@@ -330,25 +382,29 @@
     ids_t, sc_t = expert_ids.T, gate_scores.T
     perm = jnp.asarray(PERM, BF)
     big = NEXP * PEER
-    packed = pl.pallas_call(
-        pack_kernel,
-        name="pack",
-        out_shape=sd((big, LANES), BF),
-        in_specs=[vm] * 8,
-        out_specs=vm,
-        scratch_shapes=[pltpu.VMEM((2 * PIECES * TOK, LANES), BF)],
-        compiler_params=pltpu.CompilerParams(vmem_limit_bytes=48 << 20),
-    )(tokens, out_grad, expert_ids, ids_t, sc_t, jnp.asarray(BASE), jnp.asarray(ISCOT), jnp.asarray(BLOCKMASK, BF))
     wg, wu, wd = gate_proj[0], up_proj[0], down_proj[0]
     received, fg, fu, fd = pl.pallas_call(
         dispatch_kernel,
         name="dispatch",
         out_shape=(sd((NEXP, PEER, LANES), BF),) + (sd((FF, D), BF),) * 3,
-        in_specs=[anyw] * 4,
+        in_specs=[anyw] * 7,
         out_specs=(anyw,) * 4,
-        scratch_shapes=[reg((6,)), dma, dma, dma((4,)), dma((4, 3)), dma((4, 3))],
-        compiler_params=pltpu.CompilerParams(collective_id=1, has_side_effects=True, vmem_limit_bytes=16 << 20),
-    )(packed.reshape(NEXP, PEER, LANES), wg, wu, wd)
+        scratch_shapes=[
+            reg((6,)),
+            dma,
+            dma,
+            dma((8,)),
+            dma((4, 3)),
+            dma((4, 3)),
+            pltpu.VMEM((TOK, D), BF),
+            pltpu.VMEM((TOK, D), BF),
+            pltpu.VMEM((2, TOK), I32),
+            pltpu.VMEM((2, TOK), F32),
+            pltpu.VMEM((2 * PIECES * TOK, LANES), BF),
+            pltpu.VMEM((NEXP, PEER, LANES), BF),
+        ],
+        compiler_params=pltpu.CompilerParams(collective_id=1, has_side_effects=True, vmem_limit_bytes=62 << 20),
+    )(tokens, out_grad, ids_t, sc_t, wg, wu, wd)
     wspec = pl.BlockSpec((FCHUNK, D), lambda i: (i, 0))
     whole = lambda *shape: pl.BlockSpec(shape, lambda i: (0, 0))
     back, pg, pu, pd = pl.pallas_call(
@@ -361,36 +417,45 @@
         scratch_shapes=[pltpu.VMEM((SLOTS, D), BF)] * 2 + [pltpu.VMEM((SLOTS, D), F32)] * 2,
         compiler_params=pltpu.CompilerParams(vmem_limit_bytes=60 << 20),
     )(received.reshape(big, LANES), perm, fg, fu, fd)
-    returned, gg, gu, gd = pl.pallas_call(
+    returned, frm = pl.pallas_call(
         return_kernel,
         name="giveback",
-        out_shape=(sd((NEXP, PEER, LANES), BF),) + (sd((SH, D), BF),) * 3,
+        out_shape=(sd((NEXP, PEER, LANES), BF), sd((2, 3, SH, D), BF)),
         in_specs=[anyw] * 4,
-        out_specs=(anyw, vm, vm, vm),
+        out_specs=(anyw, anyw),
         scratch_shapes=[
             reg((6,)),
             dma,
             dma,
-            dma((10,)),
+            dma((7,)),
             pltpu.VMEM((2, 3, HALF, D), BF),
             pltpu.VMEM((2, 3, HALF, D), BF),
             pltpu.VMEM((2, 3, HALF, D), BF),
-            pltpu.VMEM((2, 3, SH, D), BF),
-            pltpu.VMEM((3, SH, D), BF),
             dma((6, 3)),
             dma((6, 3)),
         ],
-        compiler_params=pltpu.CompilerParams(collective_id=2, has_side_effects=True, vmem_limit_bytes=48 << 20),
+        compiler_params=pltpu.CompilerParams(collective_id=2, has_side_effects=True, vmem_limit_bytes=62 << 20),
     )(back.reshape(NEXP, PEER, LANES), pg, pu, pd)
-    output, d_tokens, d_scores = pl.pallas_call(
+    output, d_tokens, d_scores_t, gg, gu, gd = pl.pallas_call(
         combine_kernel,
         name="combine",
-        out_shape=(sd((TOK, D), BF), sd((TOK, D), BF), sd((TOK, 2), F32)),
-        in_specs=[vm] * 6,
-        out_specs=(vm,) * 3,
-        scratch_shapes=[pltpu.VMEM((SLOTS, D), BF)] * 2,
-        compiler_params=pltpu.CompilerParams(vmem_limit_bytes=48 << 20),
-    )(returned.reshape(big, LANES), perm, out_grad, expert_ids, ids_t, gate_scores)
+        out_shape=(sd((TOK, D), BF), sd((TOK, D), BF), sd((2, TOK), F32)) + (sd((SH, D), BF),) * 3,
+        in_specs=[anyw] * 9,
+        out_specs=(vm,) * 3 + (anyw,) * 3,
+        scratch_shapes=[
+            pltpu.VMEM((big, LANES), BF),
+            pltpu.VMEM((2, 3, SH, D), BF),
+            pltpu.VMEM((GROWS, GROWS), BF),
+            pltpu.VMEM((TOK, D), BF),
+            pltpu.VMEM((2, TOK), I32),
+            pltpu.VMEM((2, TOK), F32),
+        ]
+        + [pltpu.VMEM((SLOTS, D), BF)] * 2
+        + [pltpu.VMEM((3, SH, D), BF)] * 2
+        + [dma((16,)), dma((4,))],
+        compiler_params=pltpu.CompilerParams(vmem_limit_bytes=62 << 20),
+    )(returned.reshape(big, LANES), frm, perm, out_grad, ids_t, sc_t, pg, pu, pd)
+    d_scores = d_scores_t.T
     return output, d_tokens, d_scores, gg[None], gu[None], gd[None]
 
 

time: 254 us -> 221 us (0.87)
  local copies, waits for them, and re-layouts: 26.4 us -> 0 us
  Pallas kernels: 227 us -> 220 us
    unnamed x54 -> x0, local copies, waits for them, and re-layouts: 26.4 us -> none
    pallas_call x1, Pallas kernels: 96.9 us -> 91.6 us  [shards(): pl.pallas_call(dispatch_kernel, name='dispatch', out_shape=(sd((NEXP, PEE...]
    pallas_call x1 -> x0, Pallas kernels: 5.09 us -> none  [shards(): pl.pallas_call(pack_kernel, name='pack', out_shape=sd((big, LANES), BF),...]
    pallas_call x1, Pallas kernels: 5.2 us -> 8.88 us  [shards(): pl.pallas_call(combine_kernel, name='combine', out_shape=(sd((TOK, D), BF...]
where the time goes in v2:
time: 221 us; the launch traced here: 220 us
  Pallas kernels  220 us (100%)
    pallas_call x1, Pallas kernels, shards(): pl.pallas_call(dispatch_kernel, name='dispatch', out_shape=(sd((NEXP, PEE...  91.6 us
    pallas_call x1, Pallas kernels, shards(): pl.pallas_call(return_kernel, name='giveback', out_shape=(sd((NEXP, PEER,...  89.6 us
    pallas_call x1, Pallas kernels, shards(): pl.pallas_call(expert_kernel, name='expert', grid=(FF // FCHUNK,), out_sh...  29.6 us
    pallas_call x1, Pallas kernels, shards(): pl.pallas_call(combine_kernel, name='combine', out_shape=(sd((TOK, D), BF...  8.88 us

profile of v2, /device:TPU:1, one launch (start us, length us, event | category | flops | bytes accessed | tf_op | source)
XLA Modules:
  0.0 220.4 jit_solution(2333219609035888863)
XLA Ops:
  0.6 91.6 %dispatch.1 = (bf16[64,48,512]{2,1,0:T(8,128)(2,1)}, bf16[768,2048]{1,0:T(8,128)(2,1)}, bf16[768,2048]{1,0:T(8,128)(2,1)}, bf16[768,2048]{1,0:T(8,128)(2,1)}) custom-call(bf16[128,2048]{1,0:T(8,128)(2,1)} %tok.1, bf16[128,2048]{1,0:T(8,128)(2,1)} %grad_h.1, s32[2,128]{1,0:T(2,128)} %bitcast.18, f32[2,128]{1,0:T(2,128)} %bitcast.20, ...), custom_call_target="tpu_custom_call" | custom-call | tf_op jit(solution)/shard_map/dispatch/pallas_call | solution.py:386
  92.2 29.6 %expert.1 = (bf16[3072,512]{1,0:T(8,128)(2,1)}, bf16[768,2048]{1,0:T(8,128)(2,1)}, bf16[768,2048]{1,0:T(8,128)(2,1)}, bf16[768,2048]{1,0:T(8,128)(2,1)}) custom-call(bf16[3072,512]{1,0:T(8,128)(2,1)} %bitcast.14, bf16[384,384]{1,0:T(8,128)(2,1)} %constant.2.clone.perm.perm_h, bf16[768,2048]{1,0:T(8,128)(2,1)} %get-tuple-element.23.wg, ...), custom_call_target="tpu_custom_call" | custom-call | tf_op jit(solution)/shard_map/expert/pallas_call | solution.py:410
  121.8 89.6 %giveback.1 = (bf16[64,48,512]{2,1,0:T(8,128)(2,1)}, bf16[2,3,192,2048]{3,2,1,0:T(8,128)(2,1)}) custom-call(bf16[64,48,512]{2,1,0:T(8,128)(2,1)} %bitcast.13, bf16[768,2048]{1,0:T(8,128)(2,1)} %get-tuple-element.27.pg, bf16[768,2048]{1,0:T(8,128)(2,1)} %get-tuple-element.28.pu, bf16[768,2048]{1,0:T(8,128)(2,1)} %get-tuple-element.29.pd), custom_call_target="tpu_custom_call" | custom-call | tf_op jit(solution)/shard_map/giveback/pallas_call | solution.py:420
  211.4 8.9 %combine.1 = (bf16[128,2048]{1,0:T(8,128)(2,1)}, bf16[128,2048]{1,0:T(8,128)(2,1)}, f32[2,128]{1,0:T(2,128)}, bf16[192,2048]{1,0:T(8,128)(2,1)}, bf16[192,2048]{1,0:T(8,128)(2,1)}, /*index=5*/bf16[192,2048]{1,0:T(8,128)(2,1)}) custom-call(bf16[3072,512]{1,0:T(8,128)(2,1)} %bitcast.12, bf16[2,3,192,2048]{3,2,1,0:T(8,128)(2,1)} %get-tuple-element.31.frm_h, ...), custom_call_target="tpu_custom_call" | custom-call | tf_op jit(solution)/shard_map/combine/pallas_call | solution.py:439

commit v3 on v2

--- a/solution.py
+++ b/solution.py
@@ -193,25 +193,19 @@
     lax.fori_loop(start, stop, one, 0)
 
 
-def pack_rows(perm, out, first, second):
+def pack_rows(perm, out, first, second, start, stop):
     def one(g, carry):
         at = pl.ds(pl.multiple_of(g * GSLOTS, GSLOTS), GSLOTS)
-        z = [
-            ref[at, piece * LANES : (piece + 1) * LANES].astype(BF)
-            for ref in (first, second)
-            for piece in range(PIECES)
-        ]
+        z = [ref[at, piece * LANES : (piece + 1) * LANES] for ref in (first, second) for piece in range(PIECES)]
         packed = dot(perm[...], jnp.concatenate(z, axis=0), 0, 0)
-        out[pl.ds(pl.multiple_of(g * GROWS, GROWS), GROWS), :] = packed.astype(BF)
+        out[pl.ds(g * GRP, GRP)] = packed.astype(BF).reshape(GRP, PEER, LANES)
         return carry
 
-    lax.fori_loop(0, NEXP // GRP, one, 0)
-
-
-def expert_kernel(rows, perm, wg, wu, wd, out, dg, du, dd, xt, xc, acc_o, acc_i):
-    step = pl.program_id(0)
-
-    @pl.when(step == 0)
+    lax.fori_loop(start, stop, one, 0)
+
+
+def expert_kernel(rows, perm, wg, wu, wd, hid, gg, ug, dg, du, dd, xt, xc):
+    @pl.when(pl.program_id(0) == 0)
     def _():
         unpack_rows(perm, rows, xt, xc)
 
@@ -223,63 +217,82 @@
     hidden = (act * up).astype(BF)
     ggrad = (hg * up * (s * (1.0 + gate * (1.0 - s)))).astype(BF)
     ugrad = (hg * act).astype(BF)
+    hid[...], gg[...], ug[...] = hidden, ggrad, ugrad
     dg[...] = dot(ggrad, xt[...], 0, 0).astype(BF)
     du[...] = dot(ugrad, xt[...], 0, 0).astype(BF)
     dd[...] = dot(hidden, xc[...], 0, 0).astype(BF)
-    o = dot(hidden, wd[...])
-    i = dot(ggrad, wg[...]) + dot(ugrad, wu[...])
-
-    @pl.when(step == 0)
-    def _():
-        acc_o[...] = o
-        acc_i[...] = i
-
-    @pl.when(step > 0)
-    def _():
-        acc_o[...] += o
-        acc_i[...] += i
-
-    @pl.when(step == FF // FCHUNK - 1)
-    def _():
-        pack_rows(perm, out, acc_o, acc_i)
 
 
 def return_kernel(
-    x, pg, pu, pd, out, frm, bsem, xs, xr, loc, rel, add, summed, rs_s, rs_r
+    hid_h, gg_h, ug_h, wd_h, wg_h, wu_h, perm_h, pg, pu, pd,
+    out, frm,
+    bsem, xs, xr, loc, csem, rel, add, summed, rs_s, rs_r,
+    hid, gg, ug, wd, wg, wu, perm, xo, xi, x,
 ):
     me, y, *_ = place()
     up, dn, far = (y + 1) % 4, (y + 3) % 4, (y + 2) % 4
     parts = (pg, pu, pd)
     at = lambda ref, who, off, n: ref.at[pl.ds(pl.multiple_of(who * SH + off, 32), n)]
-    loads = []
-    for m, p in enumerate(parts):
-        qs = [
+    lanes = [slice(piece * LANES, (piece + 1) * LANES) for piece in range(PIECES)]
+    acts = [
+        pltpu.make_async_copy(s, d, csem.at[i])
+        for i, (s, d) in enumerate(((hid_h, hid), (gg_h, gg), (ug_h, ug), (perm_h, perm)))
+    ]
+    weights = [
+        [
+            pltpu.make_async_copy(s.at[:, cols], d.at[:, cols], csem.at[4 + 3 * piece + i])
+            for i, (s, d) in enumerate(((wd_h, wd), (wg_h, wg), (wu_h, wu)))
+        ]
+        for piece, cols in enumerate(lanes)
+    ]
+    loads = [
+        [
             pltpu.make_async_copy(at(p, up, 0, HALF), add.at[0, m], loc.at[1 + m]),
             pltpu.make_async_copy(at(p, dn, HALF, HALF), add.at[1, m], loc.at[4 + m]),
         ]
-        for q in qs:
-            q.start()
-        loads.append(qs)
-    barrier(bsem)
+        for m, p in enumerate(parts)
+    ]
+    for q in acts + sum(weights, []) + sum(loads, []):
+        q.start()
     tos = (up, dn)
     relays, directs, sums = [], [], []
-    for m, p in enumerate(parts):
-        for way in range(2):
-            q = remote(at(p, far, way * HALF, HALF), rel.at[way, m], rs_s.at[way, m], rs_r.at[way, m], (me, tos[way]))
-            q.start()
-            relays.append((m, way, q))
-    for m, p in enumerate(parts):
-        for way in range(2):
-            off = (1 - way) * HALF
-            q = remote(
-                at(p, tos[way], off, HALF),
-                frm.at[way, m, pl.ds(off, HALF)],
-                rs_s.at[2 + way, m],
-                rs_r.at[2 + way, m],
-                (me, tos[way]),
-            )
-            q.start()
-            directs.append(q)
+
+    def scatter():
+        for m, p in enumerate(parts):
+            for way in range(2):
+                q = remote(
+                    at(p, far, way * HALF, HALF), rel.at[way, m], rs_s.at[way, m], rs_r.at[way, m], (me, tos[way])
+                )
+                q.start()
+                relays.append((m, way, q))
+        for m, p in enumerate(parts):
+            for way in range(2):
+                off = (1 - way) * HALF
+                q = remote(
+                    at(p, tos[way], off, HALF),
+                    frm.at[way, m, pl.ds(off, HALF)],
+                    rs_s.at[2 + way, m],
+                    rs_r.at[2 + way, m],
+                    (me, tos[way]),
+                )
+                q.start()
+                directs.append(q)
+
+    def compute(i):
+        if i == 0:
+            for q in acts:
+                q.wait()
+        if i < PIECES:
+            for q in weights[i]:
+                q.wait()
+            cols = lanes[i]
+            xo[:, cols] = dot(hid[...], wd[:, cols]).astype(BF)
+            xi[:, cols] = (dot(gg[...], wg[:, cols]) + dot(ug[...], wu[:, cols])).astype(BF)
+        else:
+            half = NEXP // GRP // 2
+            pack_rows(perm, x, xo, xi, (i - PIECES) * half, (i - PIECES + 1) * half)
+
+    barrier(bsem, scatter, compute)
     own = start_exchange(x, out, xs, xr, loc.at[0])
     for m, way, q in relays:
         q.wait_recv()
@@ -406,36 +419,34 @@
         compiler_params=pltpu.CompilerParams(collective_id=1, has_side_effects=True, vmem_limit_bytes=62 << 20),
     )(tokens, out_grad, ids_t, sc_t, wg, wu, wd)
     wspec = pl.BlockSpec((FCHUNK, D), lambda i: (i, 0))
+    hspec = pl.BlockSpec((SLOTS, FCHUNK), lambda i: (0, i))
     whole = lambda *shape: pl.BlockSpec(shape, lambda i: (0, 0))
-    back, pg, pu, pd = pl.pallas_call(
+    hid, ggrad, ugrad, pg, pu, pd = pl.pallas_call(
         expert_kernel,
         name="expert",
         grid=(FF // FCHUNK,),
-        out_shape=(sd((big, LANES), BF),) + (sd((FF, D), BF),) * 3,
+        out_shape=(sd((SLOTS, FF), BF),) * 3 + (sd((FF, D), BF),) * 3,
         in_specs=[whole(big, LANES), whole(GROWS, GROWS)] + [wspec] * 3,
-        out_specs=(whole(big, LANES),) + (wspec,) * 3,
-        scratch_shapes=[pltpu.VMEM((SLOTS, D), BF)] * 2 + [pltpu.VMEM((SLOTS, D), F32)] * 2,
-        compiler_params=pltpu.CompilerParams(vmem_limit_bytes=60 << 20),
+        out_specs=(hspec,) * 3 + (wspec,) * 3,
+        scratch_shapes=[pltpu.VMEM((SLOTS, D), BF)] * 2,
+        compiler_params=pltpu.CompilerParams(vmem_limit_bytes=62 << 20),
     )(received.reshape(big, LANES), perm, fg, fu, fd)
     returned, frm = pl.pallas_call(
         return_kernel,
         name="giveback",
         out_shape=(sd((NEXP, PEER, LANES), BF), sd((2, 3, SH, D), BF)),
-        in_specs=[anyw] * 4,
+        in_specs=[anyw] * 10,
         out_specs=(anyw, anyw),
-        scratch_shapes=[
-            reg((6,)),
-            dma,
-            dma,
-            dma((7,)),
-            pltpu.VMEM((2, 3, HALF, D), BF),
-            pltpu.VMEM((2, 3, HALF, D), BF),
-            pltpu.VMEM((2, 3, HALF, D), BF),
-            dma((6, 3)),
-            dma((6, 3)),
-        ],
+        scratch_shapes=[reg((6,)), dma, dma, dma((7,)), dma((16,))]
+        + [pltpu.VMEM((2, 3, HALF, D), BF)] * 3
+        + [dma((6, 3)), dma((6, 3))]
+        + [pltpu.VMEM((SLOTS, FF), BF)] * 3
+        + [pltpu.VMEM((FF, D), BF)] * 3
+        + [pltpu.VMEM((GROWS, GROWS), BF)]
+        + [pltpu.VMEM((SLOTS, D), BF)] * 2
+        + [pltpu.VMEM((NEXP, PEER, LANES), BF)],
         compiler_params=pltpu.CompilerParams(collective_id=2, has_side_effects=True, vmem_limit_bytes=62 << 20),
-    )(back.reshape(NEXP, PEER, LANES), pg, pu, pd)
+    )(hid, ggrad, ugrad, fd, fg, fu, perm, pg, pu, pd)
     output, d_tokens, d_scores_t, gg, gu, gd = pl.pallas_call(
         combine_kernel,
         name="combine",

time: 221 us -> 204 us (0.923)
  Pallas kernels: 220 us -> 203 us
    pallas_call x1, Pallas kernels: 29.6 us -> 19.5 us  [shards(): pl.pallas_call(expert_kernel, name='expert', grid=(FF // FCHUNK,), out_sh...]
    pallas_call x1, Pallas kernels: 89.6 us -> 83.4 us  [shards(): pl.pallas_call(return_kernel, name='giveback', out_shape=(sd((NEXP, PEER,...]
where the time goes in v3:
time: 204 us
  Pallas kernels  203 us (100%)
    pallas_call x1, Pallas kernels, shards(): pl.pallas_call(dispatch_kernel, name='dispatch', out_shape=(sd((NEXP, PEE...  91.6 us
    pallas_call x1, Pallas kernels, shards(): pl.pallas_call(return_kernel, name='giveback', out_shape=(sd((NEXP, PEER,...  83.4 us
    pallas_call x1, Pallas kernels, shards(): pl.pallas_call(expert_kernel, name='expert', grid=(FF // FCHUNK,), out_sh...  19.5 us
    pallas_call x1, Pallas kernels, shards(): pl.pallas_call(combine_kernel, name='combine', out_shape=(sd((TOK, D), BF...  8.88 us

profile of v3, /device:TPU:1, one launch (start us, length us, event | category | flops | bytes accessed | tf_op | source)
XLA Modules:
  0.0 204.1 jit_solution(233253575196626249)
XLA Ops:
  0.6 91.6 %dispatch.1 = (bf16[64,48,512]{2,1,0:T(8,128)(2,1)}, bf16[768,2048]{1,0:T(8,128)(2,1)}, bf16[768,2048]{1,0:T(8,128)(2,1)}, bf16[768,2048]{1,0:T(8,128)(2,1)}) custom-call(bf16[128,2048]{1,0:T(8,128)(2,1)} %tok.1, bf16[128,2048]{1,0:T(8,128)(2,1)} %grad_h.1, s32[2,128]{1,0:T(2,128)} %bitcast.16, f32[2,128]{1,0:T(2,128)} %bitcast.18, ...), custom_call_target="tpu_custom_call" | custom-call | tf_op jit(solution)/shard_map/dispatch/pallas_call | solution.py:399
  92.2 19.5 %expert.1 = (bf16[384,768]{1,0:T(8,128)(2,1)}, bf16[384,768]{1,0:T(8,128)(2,1)}, bf16[384,768]{1,0:T(8,128)(2,1)}, bf16[768,2048]{1,0:T(8,128)(2,1)}, bf16[768,2...) custom-call(bf16[3072,512]{1,0:T(8,128)(2,1)} %bitcast.12, bf16[384,384]{1,0:T(8,128)(2,1)} %constant.2.clone.perm.perm_h, ...), custom_call_target="tpu_custom_call" | custom-call | tf_op jit(solution)/shard_map/expert/pallas_call | solution.py:424
  111.7 83.4 %giveback.1 = (bf16[64,48,512]{2,1,0:T(8,128)(2,1)}, bf16[2,3,192,2048]{3,2,1,0:T(8,128)(2,1)}) custom-call(bf16[384,768]{1,0:T(8,128)(2,1)} %get-tuple-element.28.hid_h, bf16[384,768]{1,0:T(8,128)(2,1)} %get-tuple-element.29.gg_h, bf16[384,768]{1,0:T(8,128)(2,1)} %get-tuple-element.30.ug_h, bf16[768,2048]{1,0:T(8,128)(2,1)} %get-tuple-element.27.wd.wd_h, ...), custom_call_target="tpu_custom_call" | custom-call | tf_op jit(solution)/shard_map/giveback/pallas_call | solution.py:434
  195.1 8.9 %combine.1 = (bf16[128,2048]{1,0:T(8,128)(2,1)}, bf16[128,2048]{1,0:T(8,128)(2,1)}, f32[2,128]{1,0:T(2,128)}, bf16[192,2048]{1,0:T(8,128)(2,1)}, bf16[192,2048]{1,0:T(8,128)(2,1)}, /*index=5*/bf16[192,2048]{1,0:T(8,128)(2,1)}) custom-call(bf16[3072,512]{1,0:T(8,128)(2,1)} %bitcast.11, bf16[2,3,192,2048]{3,2,1,0:T(8,128)(2,1)} %get-tuple-element.35.frm_h, ...), custom_call_target="tpu_custom_call" | custom-call | tf_op jit(solution)/shard_map/combine/pallas_call | solution.py:450

commit v4 on v2

v4 whole, which is shorter than its diff:
```python
import functools

import jax
import jax.numpy as jnp
import numpy as np
from jax import lax
from jax.experimental import pallas as pl
from jax.experimental.pallas import tpu as pltpu
from jax.sharding import PartitionSpec as P

MESH = pl.DeviceIdType.MESH
D, FF, TOK, CAP, NEXP, NDP = 2048, 768, 128, 6, 64, 4
SH = FF // NDP
HALF = SH // 2
SLOTS = NEXP * CAP
LANES = 512
PIECES = D // LANES
PEER = 2 * PIECES * CAP
GRP = 8
GROWS = GRP * PEER
GSLOTS = GRP * CAP
BF, F32, I32 = jnp.bfloat16, jnp.float32, jnp.int32
FCHUNK = 256

_r = np.arange(GROWS)
_peer, _kind, _piece, _slot = _r // PEER, _r % PEER // (PIECES * CAP), _r % (PIECES * CAP) // CAP, _r % CAP
_dest = (_kind * PIECES + _piece) * GSLOTS + _peer * CAP + _slot
PERM = np.zeros((GROWS, GROWS), np.float32)
PERM[_dest, _r] = 1.0


def dot(a, b, ca=1, cb=0):
    return lax.dot_general(a, b, (((ca,), (cb,)), ((), ())), preferred_element_type=F32)


def place():
    me, y = lax.axis_index("expert"), lax.axis_index("dp")
    return me, y, me // 8, (me // 2) % 4, me % 2


def tell(sem, devices):
    for d in devices:
        pl.semaphore_signal(sem, inc=1, device_id=d, device_id_type=MESH)


def barrier(sems, greeted=None, between=None):
    me, y, z, x, c = place()
    at = lambda z, x, c: z * 8 + x * 2 + c
    zs = [at((z + 1) % 8, x, c), at((z + 7) % 8, x, c)]
    xs = [at(z, (x + 1) % 4, c), at(z, (x + 3) % 4, c)]
    cs = [at(z, x, 1 - c)]
    bar = pltpu.get_barrier_semaphore()
    tell(bar, [(d, y) for d in zs + xs + cs] + [(me, (y + 1) % 4), (me, (y + 3) % 4)])
    pl.semaphore_wait(bar, 7)
    if greeted is not None:
        greeted()
    for i, group in enumerate((zs, zs, zs, xs, xs, cs)):
        tell(sems.at[i], [(d, y) for d in group])
        if between is not None:
            between(i)
        pl.semaphore_wait(sems.at[i], len(group))


def remote(src, dst, send, recv, device):
    return pltpu.make_async_remote_copy(src, dst, send, recv, device_id=device, device_id_type=MESH)


def start_exchange(src, dst, send, recv, local):
    me, y, z, x, c = place()
    own = pltpu.make_async_copy(src.at[me], dst.at[me], local)
    own.start()

    def one(k, carry):
        peer = ((z + k // 8) % 8) * 8 + ((x + (k // 2) % 4) % 4) * 2 + (c + k % 2) % 2
        remote(src.at[peer], dst.at[me], send, recv, (peer, y)).start()
        return carry

    lax.fori_loop(1, NEXP, one, 0)
    return own


def finish_exchange(src, dst, send, recv, own):
    n = NEXP - 1
    pltpu.make_async_copy(dst.at[pl.ds(0, n)], dst.at[pl.ds(0, n)], recv).wait()
    pltpu.make_async_copy(src.at[pl.ds(0, n)], src.at[pl.ds(0, n)], send).wait()
    own.wait()


def targets_row(ids, ids_t):
    before = lax.broadcasted_iota(I32, (TOK, TOK), 0) < lax.broadcasted_iota(I32, (TOK, TOK), 1)
    out = []
    for k in range(2):
        mine = ids_t[k : k + 1, :]
        same = (ids[:, 0:1] == mine).astype(F32) + (ids[:, 1:2] == mine).astype(F32)
        pos = jnp.sum(jnp.where(before, same, 0.0), axis=0, keepdims=True)
        out.append(mine * CAP + pos)
    return out


def targets_col(ids, ids_t):
    before = lax.broadcasted_iota(I32, (TOK, TOK), 1) < lax.broadcasted_iota(I32, (TOK, TOK), 0)
    out = []
    for k in range(2):
        mine = ids[:, k : k + 1]
        same = (ids_t[0:1, :] == mine).astype(F32) + (ids_t[1:2, :] == mine).astype(F32)
        pos = jnp.sum(jnp.where(before, same, 0.0), axis=1, keepdims=True)
        out.append(mine * CAP + pos)
    return out


def columns(pair):
    return jnp.concatenate([pair] * 4, axis=0).T


def pack_group(g, ids_t, ids, sc_t, out, table):
    t0, t1 = targets_row(ids, ids_t)
    s0, s1 = sc_t[0:1, :], sc_t[1:2, :]
    row = lax.broadcasted_iota(I32, (GROWS, 1), 0).astype(F32)
    six = jnp.floor((row + 0.5) * (1.0 / CAP))
    peer = jnp.floor((six + 0.5) * (1.0 / (2 * PIECES)))
    block = six - 2 * PIECES * peer
    slot = peer * CAP + (row - CAP * six) + float(g * GSLOTS)
    h0, h1 = t0 == slot, t1 == slot
    score = jnp.sum(jnp.where(h0, s0, 0.0) + jnp.where(h1, s1, 0.0), axis=1, keepdims=True)
    scale = jnp.where(block > PIECES - 0.5, score, 1.0)
    hit = h0.astype(F32) + h1.astype(F32)
    pick = jnp.concatenate([jnp.where(block == float(b), hit, 0.0).astype(BF) for b in range(2 * PIECES)], axis=1)
    rows = dot(pick, table[...]) * scale
    out[g * GRP : (g + 1) * GRP] = rows.astype(BF).reshape(GRP, PEER, LANES)


def unpack_rows(perm, rows, first, second, start=0, stop=NEXP // GRP):
    def one(g, carry):
        z = dot(perm[...], rows[pl.ds(g * GRP, GRP)].reshape(GROWS, LANES)).astype(BF)
        at = pl.ds(pl.multiple_of(g * GSLOTS, GSLOTS), GSLOTS)
        for kind, ref in enumerate((first, second)):
            for piece in range(PIECES):
                o = (kind * PIECES + piece) * GSLOTS
                ref[at, piece * LANES : (piece + 1) * LANES] = z[o : o + GSLOTS]
        return carry

    lax.fori_loop(start, stop, one, 0)


def pack_rows(perm, out, first, second, start, stop):
    def one(g, carry):
        at = pl.ds(pl.multiple_of(g * GSLOTS, GSLOTS), GSLOTS)
        z = [ref[at, piece * LANES : (piece + 1) * LANES] for ref in (first, second) for piece in range(PIECES)]
        packed = dot(perm[...], jnp.concatenate(z, axis=0), 0, 0)
        out[pl.ds(g * GRP, GRP)] = packed.astype(BF).reshape(GRP, PEER, LANES)
        return carry

    lax.fori_loop(start, stop, one, 0)


def layer_kernel(
    tok, grad, ids, sc, wg, wu, wd, perm_h,
    out, own_out, frm,
    bsem, xs, xr, loc, ws, wr, rs_s, rs_r,
    tv, gv, iv, sv, table, perm, x, rows, fg, fu, fd, xt, xc, xo, xi, hid, gg, ug, part, rel,
):
    me, y, *_ = place()
    up, dn, far = (y + 1) % 4, (y + 3) % 4, (y + 2) % 4
    tos = (up, dn)
    shards, fulls = (wg, wu, wd), (fg, fu, fd)
    span = lambda who, off, n: pl.ds(pl.multiple_of(who * SH + off, 32), n)
    loads = [
        pltpu.make_async_copy(s, d, loc.at[i])
        for i, (s, d) in enumerate(((ids, iv), (sc, sv), (tok, tv), (grad, gv), (perm_h, perm)))
    ]
    mine = [pltpu.make_async_copy(s, f.at[span(y, 0, SH)], loc.at[5 + m]) for m, (s, f) in enumerate(zip(shards, fulls))]
    for q in loads + mine:
        q.start()
    first, relay = [], []

    def gather():
        for m, (s, f) in enumerate(zip(shards, fulls)):
            for way, to in enumerate(tos):
                q = remote(s, f.at[span(y, 0, SH)], ws.at[way, m], wr.at[way, m], (me, to))
                q.start()
                first.append((m, way, q))

    def pack(i):
        if i == 0:
            for q in loads:
                q.wait()
            for piece in range(PIECES):
                lanes = slice(piece * LANES, (piece + 1) * LANES)
                table[piece * TOK : (piece + 1) * TOK, :] = tv[:, lanes]
                table[(PIECES + piece) * TOK : (PIECES + piece + 1) * TOK, :] = gv[:, lanes]
        ids_t = iv[...].astype(F32)
        for g in ((0,), (1, 2), (3, 4), (5, 6), (7,), ())[i]:
            pack_group(g, ids_t, columns(ids_t), sv[...], x, table)

    barrier(bsem, gather, pack)
    own = start_exchange(x, rows, xs.at[0], xr.at[0], loc.at[8])
    for m, way, q in first:
        q.wait_recv()
        p = fulls[m].at[span(tos[1 - way], way * HALF, HALF)]
        r = remote(p, p, ws.at[2 + way, m], wr.at[2 + way, m], (me, tos[way]))
        r.start()
        relay.append(r)
    finish_exchange(x, rows, xs.at[0], xr.at[0], own)
    unpack_rows(perm, rows, xt, xc)
    for q in relay:
        q.wait()
    for _, _, q in first:
        q.wait_send()
    for q in mine:
        q.wait()

    def units(i, carry):
        at = pl.ds(pl.multiple_of(i * FCHUNK, FCHUNK), FCHUNK)
        gate = dot(fg[at, :], xt[...], 1, 1)
        upp = dot(fu[at, :], xt[...], 1, 1)
        hg = dot(fd[at, :], xc[...], 1, 1)
        s = jax.nn.sigmoid(gate)
        act = gate * s
        hid[at, :] = (act * upp).astype(BF)
        gg[at, :] = (hg * upp * (s * (1.0 + gate * (1.0 - s)))).astype(BF)
        ug[at, :] = (hg * act).astype(BF)
        return carry

    lax.fori_loop(0, FF // FCHUNK, units, 0)

    def gradients(who):
        at = span(who, 0, SH)
        part[0, at, :] = dot(gg[at, :], xt[...]).astype(BF)
        part[1, at, :] = dot(ug[at, :], xt[...]).astype(BF)
        part[2, at, :] = dot(hid[at, :], xc[...]).astype(BF)

    def send(m, way, src, dst, row):
        q = remote(src, dst, rs_s.at[row + way, m], rs_r.at[row + way, m], (me, tos[way]))
        q.start()
        return q

    gradients(far)
    relays = [
        (m, way, send(m, way, part.at[m, span(far, way * HALF, HALF)], rel.at[way, m], 0)) for m in range(3) for way in range(2)
    ]
    for piece in range(2):
        cols = slice(piece * D // 2, (piece + 1) * D // 2)
        xo[:, cols] = dot(hid[...], fd[:, cols], 0, 0).astype(BF)
        xi[:, cols] = (dot(gg[...], fg[:, cols], 0, 0) + dot(ug[...], fu[:, cols], 0, 0)).astype(BF)
    pack_rows(perm, x, xo, xi, 0, NEXP // GRP)
    own = start_exchange(x, out, xs.at[1], xr.at[1], loc.at[9])
    gradients(up)
    gradients(dn)
    directs = []
    for m in range(3):
        for way in range(2):
            off = (1 - way) * HALF
            directs.append(send(m, way, part.at[m, span(tos[way], off, HALF)], frm.at[way, m, pl.ds(off, HALF)], 2))
    gradients(y)
    keep = pltpu.make_async_copy(part.at[:, span(y, 0, SH)], own_out, loc.at[10])
    keep.start()
    sums = []
    for m, way, q in relays:
        q.wait_recv()
        off = way * HALF

        def add_rows(r, carry):
            at = span(tos[way], off + r * 32, 32)
            total = part[m, at, :].astype(F32) + rel[way, m, pl.ds(pl.multiple_of(r * 32, 32), 32), :].astype(F32)
            part[m, at, :] = total.astype(BF)
            return carry

        lax.fori_loop(0, HALF // 32, add_rows, 0)
        sums.append(send(m, way, part.at[m, span(tos[way], off, HALF)], frm.at[way, m, pl.ds(off, HALF)], 4))
    for q in directs:
        q.wait()
    for q in sums:
        q.wait()
    for _, _, q in relays:
        q.wait_send()
    keep.wait()
    finish_exchange(x, out, xs.at[1], xr.at[1], own)


def combine_kernel(
    rows_h, frm_h, own_h, perm_h, grad_h, ids_h, sc_h,
    out, dtok, dsc, og, ou, od,
    rows, frm, perm, grad, ids, sc, xo, xi, own, fin, sem, rsem,
):
    outs = (og, ou, od)
    small = [
        pltpu.make_async_copy(s, d, sem.at[6 + i])
        for i, (s, d) in enumerate(((perm_h, perm), (grad_h, grad), (ids_h, ids), (sc_h, sc)))
    ]
    span = 2 * GRP
    chunks = [
        pltpu.make_async_copy(rows_h.at[pl.ds(i * span, span)], rows.at[pl.ds(i * span, span)], rsem.at[i]) for i in range(4)
    ]
    load = [
        [
            pltpu.make_async_copy(own_h.at[m], own.at[m], sem.at[m]),
            pltpu.make_async_copy(frm_h.at[0, m], frm.at[0, m], sem.at[10 + m]),
            pltpu.make_async_copy(frm_h.at[1, m], frm.at[1, m], sem.at[13 + m]),
        ]
        for m in range(3)
    ]
    store = [pltpu.make_async_copy(fin.at[m], o, sem.at[3 + m]) for m, o in enumerate(outs)]
    for q in small + chunks + sum(load, []):
        q.start()
    for q in small:
        q.wait()
    for i in range(4):
        chunks[i].wait()
        unpack_rows(perm, rows, xo, xi, 2 * i, 2 * i + 2)
    for m in range(3):
        for q in load[m]:
            q.wait()

        def final(r, carry):
            at = pl.ds(pl.multiple_of(r * 32, 32), 32)
            total = own[m, at, :].astype(F32) + frm[0, m, at, :].astype(F32)
            fin[m, at, :] = (total + frm[1, m, at, :].astype(F32)).astype(BF)
            return carry

        lax.fori_loop(0, SH // 32, final, 0)
        store[m].start()
    ids_t = ids[...].astype(F32)
    t0, t1 = targets_col(columns(ids_t), ids_t)
    slot = lax.broadcasted_iota(I32, (TOK, SLOTS), 1).astype(F32)
    g0 = (t0 == slot).astype(F32).astype(BF)
    g1 = (t1 == slot).astype(F32).astype(BF)
    both = g0 + g1
    sc_c = columns(sc[...])
    s0, s1 = sc_c[:, 0:1], sc_c[:, 1:2]
    d0 = jnp.zeros((TOK, 1), F32)
    d1 = jnp.zeros((TOK, 1), F32)
    for piece in range(PIECES):
        lanes = slice(piece * LANES, (piece + 1) * LANES)
        p0 = dot(g0, xo[:, lanes])
        p1 = dot(g1, xo[:, lanes])
        cot = grad[:, lanes].astype(F32)
        out[:, lanes] = (s0 * p0 + s1 * p1).astype(BF)
        d0 += jnp.sum(cot * p0, axis=1, keepdims=True)
        d1 += jnp.sum(cot * p1, axis=1, keepdims=True)
        dtok[:, lanes] = dot(both, xi[:, lanes]).astype(BF)
    dsc[...] = jnp.concatenate([d0, d1] * 4, axis=1).T[0:2, :]
    for q in store:
        q.wait()


def shards(tokens, expert_ids, gate_scores, gate_proj, up_proj, down_proj, out_grad):
    sd, vmem = jax.ShapeDtypeStruct, pltpu.VMEM
    vm = pl.BlockSpec(memory_space=pltpu.VMEM)
    anyw = pl.BlockSpec(memory_space=pl.ANY)
    dma, reg = pltpu.SemaphoreType.DMA, pltpu.SemaphoreType.REGULAR
    ids_t, sc_t = expert_ids.T, gate_scores.T
    perm = jnp.asarray(PERM, BF)
    blocks = (NEXP, PEER, LANES)
    returned, own, frm = pl.pallas_call(
        layer_kernel,
        name="layer",
        out_shape=(sd(blocks, BF), sd((3, SH, D), BF), sd((2, 3, SH, D), BF)),
        in_specs=[anyw] * 8,
        out_specs=(anyw,) * 3,
        scratch_shapes=[reg((6,)), dma((2,)), dma((2,)), dma((11,)), dma((4, 3)), dma((4, 3)), dma((6, 3)), dma((6, 3))]
        + [vmem((TOK, D), BF)] * 2
        + [vmem((2, TOK), I32), vmem((2, TOK), F32), vmem((2 * PIECES * TOK, LANES), BF), vmem((GROWS, GROWS), BF)]
        + [vmem(blocks, BF)] * 2
        + [vmem((FF, D), BF)] * 3
        + [vmem((SLOTS, D), BF)] * 4
        + [vmem((FF, SLOTS), BF)] * 3
        + [vmem((3, FF, D), BF), vmem((2, 3, HALF, D), BF)],
        compiler_params=pltpu.CompilerParams(collective_id=1, has_side_effects=True, vmem_limit_bytes=63 << 20),
    )(tokens, out_grad, ids_t, sc_t, gate_proj[0], up_proj[0], down_proj[0], perm)
    output, d_tokens, d_scores_t, gg, gu, gd = pl.pallas_call(
        combine_kernel,
        name="combine",
        out_shape=(sd((TOK, D), BF), sd((TOK, D), BF), sd((2, TOK), F32)) + (sd((SH, D), BF),) * 3,
        in_specs=[anyw] * 7,
        out_specs=(vm,) * 3 + (anyw,) * 3,
        scratch_shapes=[vmem(blocks, BF), vmem((2, 3, SH, D), BF), vmem((GROWS, GROWS), BF), vmem((TOK, D), BF)]
        + [vmem((2, TOK), I32), vmem((2, TOK), F32)]
        + [vmem((SLOTS, D), BF)] * 2
        + [vmem((3, SH, D), BF)] * 2
        + [dma((16,)), dma((4,))],
        compiler_params=pltpu.CompilerParams(vmem_limit_bytes=62 << 20),
    )(returned, frm, own, perm, out_grad, ids_t, sc_t)
    return output, d_tokens, d_scores_t.T, gg[None], gu[None], gd[None]


def solution(mesh):
    rows, weights = P(("expert", "dp"), None), P("expert", "dp", None)
    return jax.shard_map(
        shards,
        mesh=mesh,
        in_specs=(rows, rows, rows, weights, weights, weights, rows),
        out_specs=(rows, rows, rows, weights, weights, weights),
        check_vma=False,
    )
```

time: 221 us -> 196 us (0.89)
  Pallas kernels: 220 us -> 194 us
    pallas_call x3 -> x1, Pallas kernels: 211 us -> 185 us  [shards(): pl.pallas_call(layer_kernel, name='layer', out_shape=(sd(blocks, BF), sd(...]
where the time goes in v4:
time: 196 us; the launch traced here: 195 us
  Pallas kernels  194 us (99%)
    pallas_call x1, Pallas kernels, shards(): pl.pallas_call(layer_kernel, name='layer', out_shape=(sd(blocks, BF), sd(...  185 us
    pallas_call x1, Pallas kernels, shards(): pl.pallas_call(combine_kernel, name='combine', out_shape=(sd((TOK, D), BF...  9.15 us

profile of v4, /device:TPU:1, one launch (start us, length us, event | category | flops | bytes accessed | tf_op | source)
XLA Modules:
  0.0 194.7 jit_solution(8860313568634642120)
XLA Ops:
  0.6 184.8 %layer.1 = (bf16[64,48,512]{2,1,0:T(8,128)(2,1)}, bf16[3,192,2048]{2,1,0:T(8,128)(2,1)}, bf16[2,3,192,2048]{3,2,1,0:T(8,128)(2,1)}) custom-call(bf16[128,2048]{1,0:T(8,128)(2,1)} %tok.1, bf16[128,2048]{1,0:T(8,128)(2,1)} %grad_h.1, s32[2,128]{1,0:T(2,128)} %bitcast.12, f32[2,128]{1,0:T(2,128)} %bitcast.14, bf16[192,2048]{1,0:T(8,128)(2,1)} %bitcast.9, ...), custom_call_target="tpu_custom_call" | custom-call | tf_op jit(solution)/shard_map/layer/pallas_call | solution.py:354
  185.4 9.1 %combine.1 = (bf16[128,2048]{1,0:T(8,128)(2,1)}, bf16[128,2048]{1,0:T(8,128)(2,1)}, f32[2,128]{1,0:T(2,128)}, bf16[192,2048]{1,0:T(8,128)(2,1)}, bf16[192,2048]{1,0:T(8,128)(2,1)}, /*index=5*/bf16[192,2048]{1,0:T(8,128)(2,1)}) custom-call(bf16[64,48,512]{2,1,0:T(8,128)(2,1)} %get-tuple-element.15.rows_h, bf16[2,3,192,2048]{3,2,1,0:T(8,128)(2,1)} %get-tuple-element.16.frm_h, ...), custom_call_target="tpu_custom_call" | custom-call | tf_op jit(solution)/shard_map/combine/pallas_call | solution.py:370
